TPU v7x, 32 devices: a whole 2x2x4 slice. The times are simulated.
32 devices in a mesh: ctx: 8 (over y, x, core), fsdp: 4 (over z).
Axes of the slice: x: 2, y: 2, z: 4, core: 2. Of those that a mesh axis runs over, the one named last changes fastest.
Arguments:
- tokens: bfloat16 [4, 2048, 1536], P('fsdp', 'ctx'), may hold values from -6 to 6
- cotangent: bfloat16 [4, 2048, 1536], P('fsdp', 'ctx'), may hold values from -6 to 6
- attend_gain: bfloat16 [1536], P('fsdp'), may hold values from 0.5 to 1.5
- w_query: bfloat16 [1536, 1536], P('fsdp'), may hold values from -0.21875 to 0.21875
- w_key: bfloat16 [1536, 768], P('fsdp'), may hold values from -0.15625 to 0.15625
- w_value: bfloat16 [1536, 768], P('fsdp'), may hold values from -0.15625 to 0.15625
- w_out: bfloat16 [1536, 1536], P('fsdp'), may hold values from -2 to 2
- feed_gain: bfloat16 [1536], P('fsdp'), may hold values from 0.5 to 1.5
- w_gate: bfloat16 [1536, 4096], P('fsdp'), may hold values from -0.15625 to 0.15625
- w_up: bfloat16 [1536, 4096], P('fsdp'), may hold values from -0.15625 to 0.15625
- w_down: bfloat16 [4096, 1536], P('fsdp'), may hold values from -0.1875 to 0.1875
- lengths: int32 [4], P('fsdp'), may hold values from 512 to 2048, as said below
- deal_table: int32 [16], replicated, may hold values from 0 to 15, as said below
Outputs:
- layer_out: bfloat16 [4, 2048, 1536], P('fsdp', 'ctx')
- grad_tokens: float32 [4, 2048, 1536], P('fsdp', 'ctx')
- grad_attend_gain: float32 [1536], P('fsdp')
- grad_query: float32 [1536, 1536], P('fsdp')
- grad_key: float32 [1536, 768], P('fsdp')
- grad_value: float32 [1536, 768], P('fsdp')
- grad_out: float32 [1536, 1536], P('fsdp')
- grad_feed_gain: float32 [1536], P('fsdp')
- grad_gate: float32 [1536, 4096], P('fsdp')
- grad_up: float32 [1536, 4096], P('fsdp')
- grad_down: float32 [4096, 1536], P('fsdp')
- rms_stats: float32 [4, 3], P('fsdp')
Inputs may be any that keep to these rules, and one draw needn't show every extreme that they name: Slot s holds valid tokens at sequence positions 0 to lengths[s] - 1, the rest is padding; in every draw some slot is full with 2048. Stored block b of every slot holds the tokens of sequence block deal_table[b]; the table is a permutation, and entries 2c and 2c + 1 sum to 15.
All inputs are finite; a program needn't handle non-finite values.
Results may differ from a plain program's by a relative error of at most 0.015.
Values may be sent and summed in bfloat16 or wider, within the bound.
No kernel may reach another device: no remote copies, remote signals or barrier semaphores. Data moves between devices by JAX's collectives and lax.ppermute only.
A program may use at most 320 MiB of HBM per device.

v0:
```python
import functools
import math

import jax
import jax.numpy as jnp
from jax import lax
from jax.experimental import pallas as pl
from jax.experimental.pallas import tpu as pltpu
from jax.sharding import PartitionSpec as P


D = 1536
QUERY_HEADS = 16
KEY_VALUE_HEADS = 8
HEAD_WIDTH = 96
HALF = HEAD_WIDTH // 2
BLK = 128
LANES = 128

EPS = 1e-05
ROPE_BASE = 10000.0
NEG = -1e30
SCALE = 1.0 / math.sqrt(HEAD_WIDTH)
TILE = 256
CHUNKS = 4

F32 = jnp.float32
BF16 = jnp.bfloat16


def dot(left, right):
    return lax.dot_general(left, right, (((1,), (0,)), ((), ())), preferred_element_type=F32)


def dot_t(left, right):
    return lax.dot_general(left, right, (((1,), (1,)), ((), ())), preferred_element_type=F32)


def dot_outer(left, right):
    return lax.dot_general(left, right, (((0,), (0,)), ((), ())), preferred_element_type=F32)


def turn(rows, cos_rows, sin_rows):
    return rows * cos_rows + pltpu.roll(rows, LANES // 2, 1) * sin_rows


def mask_tile(scores, key_start, query_start, length):
    key_pos = key_start + lax.broadcasted_iota(jnp.int32, scores.shape, 0)
    query_pos = query_start + lax.broadcasted_iota(jnp.int32, scores.shape, 1)
    return jnp.where((key_pos <= query_pos) & (key_pos < length), scores, NEG)


def attend_kernel(heads, table, length_ref, *refs):
    raws, rest = refs[:CHUNKS], refs[CHUNKS:]
    cos_t, sin_t, ctx_low, query_s, key_s, value_s, ctx_s, lse_s, value_t, score_s = rest
    rows_all = key_s.shape[0]
    piece = raws[0].shape[0] // BLK
    length = length_ref[0]

    for k, raw in enumerate(raws):

        @pl.loop(0, piece)
        def _(b, k=k, raw=raw):
            src = pl.ds(pl.multiple_of(b * BLK, BLK), BLK)
            here = pl.ds(pl.multiple_of((k * piece + b) * BLK, BLK), BLK)
            dst = pl.ds(pl.multiple_of(table[k * piece + b] * BLK, BLK), BLK)
            cos_rows = cos_t[here, :]
            sin_rows = sin_t[here, :]
            for h in range(heads):
                part = raw[src, h * LANES : (h + 1) * LANES]
                query_s[h, dst, :] = turn(part, cos_rows, sin_rows).astype(BF16)
            part = raw[src, heads * LANES : (heads + 1) * LANES]
            key_s[dst, :] = turn(part, cos_rows, sin_rows).astype(BF16)
            part = raw[src, (heads + 1) * LANES : (heads + 2) * LANES]
            value_s[dst, :] = part.astype(BF16)
            value_t[:, dst] = part.T.astype(BF16)

    every = range(heads)

    @pl.loop(0, rows_all // TILE)
    def _(i):
        q_rows = pl.ds(pl.multiple_of(i * TILE, TILE), TILE)
        full = jnp.minimum(i, length // TILE)

        def score(j, tops, masked):
            k_rows = pl.ds(pl.multiple_of(j * TILE, TILE), TILE)
            key = key_s[k_rows, :]
            out = []
            for h in every:
                tile = dot_t(key, query_s[h, q_rows, :])
                if masked:
                    tile = mask_tile(tile, j * TILE, i * TILE, length)
                score_s[h, k_rows, :] = tile
                out.append(jnp.maximum(tops[h], jnp.max(tile, axis=0, keepdims=True)))
            return tuple(out)

        tops = tuple(jnp.full((1, TILE), NEG, F32) for _ in every)
        tops = lax.fori_loop(0, full, lambda j, t: score(j, t, False), tops)
        tops = lax.fori_loop(full, i + 1, lambda j, t: score(j, t, True), tops)

        def accumulate(j, carry):
            k_rows = pl.ds(pl.multiple_of(j * TILE, TILE), TILE)
            out = []
            for h in every:
                total, context = carry[h]
                weight = jnp.exp((score_s[h, k_rows, :] - tops[h]) * SCALE)
                total = total + jnp.sum(weight, axis=0, keepdims=True)
                context = context + dot(value_t[:, k_rows], weight.astype(BF16))
                out.append((total, context))
            return tuple(out)

        start = tuple((jnp.zeros((1, TILE), F32), jnp.zeros((LANES, TILE), F32)) for _ in every)
        sums = lax.fori_loop(0, i + 1, accumulate, start)
        for h in every:
            total, context = sums[h]
            ctx_s[q_rows, h * LANES : (h + 1) * LANES] = (context / total).T
            lse_s[h, :, q_rows] = jnp.broadcast_to(tops[h] * SCALE + jnp.log(total), (8, TILE))

    @pl.loop(0, rows_all // BLK)
    def _(b):
        dst = pl.ds(pl.multiple_of(b * BLK, BLK), BLK)
        src = pl.ds(pl.multiple_of(table[b] * BLK, BLK), BLK)
        ctx_low[dst, :] = ctx_s[src, :].astype(BF16)


def attend(table, length, raws, cos_t, sin_t, heads):
    rows_all = cos_t.shape[0]
    smem = pl.BlockSpec(memory_space=pltpu.SMEM)
    vmem = pl.BlockSpec(memory_space=pltpu.VMEM)
    pairs = heads * rows_all * rows_all // 2
    return pl.pallas_call(
        functools.partial(attend_kernel, heads),
        out_shape=(
            jax.ShapeDtypeStruct((rows_all, heads * LANES), BF16),
            jax.ShapeDtypeStruct((heads, rows_all, LANES), BF16),
            jax.ShapeDtypeStruct((rows_all, LANES), BF16),
            jax.ShapeDtypeStruct((rows_all, LANES), BF16),
            jax.ShapeDtypeStruct((rows_all, heads * LANES), F32),
            jax.ShapeDtypeStruct((heads, 8, rows_all), F32),
        ),
        in_specs=[smem, smem] + [vmem] * (CHUNKS + 2),
        out_specs=(vmem,) * 6,
        scratch_shapes=[
            pltpu.VMEM((LANES, rows_all), BF16),
            pltpu.VMEM((heads, rows_all, TILE), F32),
        ],
        compiler_params=pltpu.CompilerParams(vmem_limit_bytes=48 << 20),
        cost_estimate=pl.CostEstimate(
            flops=4 * pairs * LANES, transcendentals=pairs, bytes_accessed=rows_all * 8192
        ),
        name="attend",
    )(table, length, *raws, cos_t, sin_t)


def attend_back_kernel(heads, table, length_ref, query_s, key_s, value_s, ctx_s, lse_s, *refs):
    backs, rest = refs[: 2 * CHUNKS], refs[2 * CHUNKS :]
    cos_t, sin_t, out, back_s, delta_s, key_t, query_acc, key_all, value_all = rest
    rows_all = key_s.shape[0]
    piece = backs[0].shape[0] // BLK
    length = length_ref[0]
    tiles = rows_all // TILE

    for k, back_low in enumerate(backs):

        @pl.loop(0, piece)
        def _(b, k=k, back_low=back_low):
            src = pl.ds(pl.multiple_of(b * BLK, BLK), BLK)
            dst = pl.ds(pl.multiple_of(table[k * piece + b] * BLK, BLK), BLK)
            for h in range(heads):
                cols = slice(h * LANES, (h + 1) * LANES)
                part = back_low[src, cols]
                back_s[h, dst, :] = part
                inner = jnp.sum(part.astype(F32) * ctx_s[dst, cols], axis=1, keepdims=True)
                delta_s[h, :, dst] = jnp.broadcast_to(inner, (BLK, BLK)).T[:8, :]

    @pl.loop(0, rows_all // BLK)
    def _(b):
        rows = pl.ds(pl.multiple_of(b * BLK, BLK), BLK)
        key_t[:, rows] = key_s[rows, :].astype(F32).T.astype(BF16)

    query_acc[...] = jnp.zeros_like(query_acc)
    key_all[...] = jnp.zeros_like(key_all)
    value_all[...] = jnp.zeros_like(value_all)

    def step(i, j, masked):
        k_rows = pl.ds(pl.multiple_of(j * TILE, TILE), TILE)
        q_rows = pl.ds(pl.multiple_of(i * TILE, TILE), TILE)
        key = key_s[k_rows, :]
        value = value_s[k_rows, :]
        value_sum = key_sum = None
        for h in range(heads):
            query = query_s[h, q_rows, :]
            back = back_s[h, q_rows, :]
            tile = dot_t(key, query)
            if masked:
                tile = mask_tile(tile, j * TILE, i * TILE, length)
            soft = jnp.exp(tile * SCALE - lse_s[h, :1, q_rows])
            back_soft = dot_t(value, back)
            low = (soft * (back_soft - delta_s[h, :1, q_rows])).astype(BF16)
            value_part = dot(soft.astype(BF16), back)
            key_part = dot(low, query)
            value_sum = value_part if h == 0 else value_sum + value_part
            key_sum = key_part if h == 0 else key_sum + key_part
            query_acc[h, :, q_rows] += dot(key_t[:, k_rows], low)
        value_all[k_rows, :] += value_sum
        key_all[k_rows, :] += key_sum

    @pl.loop(0, tiles)
    def _(i):
        full = jnp.minimum(i, length // TILE)

        @pl.loop(0, full)
        def _(j):
            step(i, j, False)

        @pl.loop(full, i + 1)
        def _(j):
            step(i, j, True)

    @pl.loop(0, rows_all // BLK)
    def _(b):
        dst = pl.ds(pl.multiple_of(b * BLK, BLK), BLK)
        src = pl.ds(pl.multiple_of(table[b] * BLK, BLK), BLK)
        cos_rows = cos_t[dst, :]
        sin_rows = -sin_t[dst, :]
        for h in range(heads):
            part = query_acc[h, :, src].T * SCALE
            out[dst, h * LANES : (h + 1) * LANES] = turn(part, cos_rows, sin_rows).astype(BF16)
        part = key_all[src, :] * SCALE
        out[dst, heads * LANES : (heads + 1) * LANES] = turn(part, cos_rows, sin_rows).astype(BF16)
        out[dst, (heads + 1) * LANES : (heads + 2) * LANES] = value_all[src, :].astype(BF16)


def attend_back(table, length, saved, backs, cos_t, sin_t, heads):
    query_s, key_s, value_s, ctx_s, lse_s = saved
    rows_all = key_s.shape[0]
    smem = pl.BlockSpec(memory_space=pltpu.SMEM)
    vmem = pl.BlockSpec(memory_space=pltpu.VMEM)
    pairs = heads * rows_all * rows_all // 2
    return pl.pallas_call(
        functools.partial(attend_back_kernel, heads),
        out_shape=jax.ShapeDtypeStruct((rows_all, (heads + 2) * LANES), BF16),
        in_specs=[smem, smem] + [vmem] * (7 + 2 * CHUNKS),
        out_specs=vmem,
        scratch_shapes=[
            pltpu.VMEM((heads, rows_all, LANES), BF16),
            pltpu.VMEM((heads, 8, rows_all), F32),
            pltpu.VMEM((LANES, rows_all), BF16),
            pltpu.VMEM((heads, LANES, rows_all), F32),
            pltpu.VMEM((rows_all, LANES), F32),
            pltpu.VMEM((rows_all, LANES), F32),
        ],
        compiler_params=pltpu.CompilerParams(vmem_limit_bytes=48 << 20),
        cost_estimate=pl.CostEstimate(
            flops=10 * pairs * LANES, transcendentals=pairs, bytes_accessed=rows_all * 8192
        ),
        name="attend_back",
    )(table, length, query_s, key_s, value_s, ctx_s, lse_s, *backs, cos_t, sin_t)


def whole_call(kernel, out_shape, args, flops, nbytes):
    vmem = pl.BlockSpec(memory_space=pltpu.VMEM)
    return pl.pallas_call(
        kernel,
        out_shape=out_shape,
        in_specs=[vmem] * len(args),
        out_specs=jax.tree.map(lambda _: vmem, out_shape),
        compiler_params=pltpu.CompilerParams(vmem_limit_bytes=48 << 20),
        cost_estimate=pl.CostEstimate(flops=flops, transcendentals=0, bytes_accessed=nbytes),
    )(*args)


def like(rows, cols, dtype):
    return jax.ShapeDtypeStruct((rows, cols), dtype)


def scale_of(rows):
    return lax.rsqrt(jnp.mean(rows * rows, axis=-1, keepdims=True) + EPS)


def project_kernel(even, odd, weight, gain, low_even, low_odd, raw):
    for source, low, start in ((even, low_even, 0), (odd, low_odd, even.shape[0])):
        for b in range(source.shape[0] // TILE):
            src = slice(b * TILE, (b + 1) * TILE)
            rows_f = source[src, :].astype(F32)
            low[src, :] = (rows_f * scale_of(rows_f) * gain[...]).astype(BF16)
            raw[start + b * TILE : start + (b + 1) * TILE, :] = dot(low[src, :], weight[...])


def project_pair(pair, weight, gain):
    rows = pair[0].shape[0]
    cols = weight.shape[1]
    out = (like(rows, D, BF16), like(rows, D, BF16), like(2 * rows, cols, F32))
    return whole_call(project_kernel, out, (*pair, weight, gain), 4 * rows * D * cols, 8 * rows * D)


def project_back_kernel(turned, weight, even, odd, sum_even, sum_odd, gain_sum):
    total = jnp.zeros((1, D), F32)
    for tokens, out, start in ((odd, sum_odd, even.shape[0]), (even, sum_even, 0)):
        for b in range(tokens.shape[0] // TILE):
            dst = slice(b * TILE, (b + 1) * TILE)
            rows_f = tokens[dst, :].astype(F32)
            part = dot_t(turned[start + b * TILE : start + (b + 1) * TILE, :], weight[...])
            out[dst, :] = part.astype(out.dtype)
            total = total + jnp.sum(part * rows_f * scale_of(rows_f), axis=0, keepdims=True)
    gain_sum[...] = jnp.broadcast_to(total, gain_sum.shape)


def project_back_pair(turned, weight, pair):
    rows = pair[0].shape[0]
    cols = weight.shape[1]
    out = (like(rows, D, F32), like(rows, D, BF16), like(8, D, F32))
    return whole_call(
        project_back_kernel, out, (turned, weight, *pair),
        4 * rows * D * cols, 10 * rows * D,
    )


def feed_kernel(
    feed_even, feed_odd, cot_even, cot_odd, live, pair_w, down_w, low_even, low_odd, hidden,
    pair_back, sum_even, sum_odd,
):
    units = down_w.shape[0]
    half = TILE
    for b in range(feed_even.shape[0] // half):
        here = slice(b * half, (b + 1) * half)
        other = slice(feed_even.shape[0] + b * half, feed_even.shape[0] + (b + 1) * half)
        low_even[here, :] = (cot_even[here, :].astype(F32) * live[here, :]).astype(BF16)
        low_odd[here, :] = (cot_odd[here, :].astype(F32) * live[other, :]).astype(BF16)
        feed = jnp.concatenate([feed_even[here, :], feed_odd[here, :]])
        low = jnp.concatenate([low_even[here, :], low_odd[here, :]])
        gate_pre = dot(feed, pair_w[:, :units])
        up_pre = dot(feed, pair_w[:, units:])
        back_hidden = dot_t(low, down_w[...])
        gate_sigmoid = jax.nn.sigmoid(gate_pre)
        gate_silu = gate_pre * gate_sigmoid
        act = (gate_silu * up_pre).astype(BF16)
        gate_back = (
            back_hidden * up_pre * gate_sigmoid * (1.0 + gate_pre * (1.0 - gate_sigmoid))
        ).astype(BF16)
        up_back = (back_hidden * gate_silu).astype(BF16)
        for rows, start in ((here, 0), (other, half)):
            hidden[rows, :] = act[start : start + half]
            pair_back[rows, :units] = gate_back[start : start + half]
            pair_back[rows, units:] = up_back[start : start + half]
        total = dot_t(jnp.concatenate([gate_back, up_back], axis=1), pair_w[...])
        sum_even[here, :] = total[:half]
        sum_odd[here, :] = total[half:].astype(BF16)


def feed_pair(feed, cot, live, pair_w, down_w):
    rows = feed[0].shape[0]
    units = down_w.shape[0]
    out = (
        like(rows, D, BF16), like(rows, D, BF16), like(2 * rows, units, BF16),
        like(2 * rows, 2 * units, BF16), like(rows, D, F32), like(rows, D, BF16),
    )
    return whole_call(
        feed_kernel, out, (*feed, *cot, live, pair_w, down_w),
        20 * rows * D * units, 20 * rows * D,
    )


def outer_kernel(count, *refs):
    lefts, rights, out = refs[:count], refs[count:-1], refs[-1]
    ratio = count // len(rights)
    rows = lefts[0].shape[0]
    cols = out.shape[1]
    step = min(cols, 512)

    tile = min(out.shape[0], TILE)

    @pl.loop(0, out.shape[0] // tile)
    def _(m):
        part = pl.ds(pl.multiple_of(m * tile, tile), tile)
        for n in range(cols // step):
            span = slice(n * step, (n + 1) * step)
            total = None
            for k, left in enumerate(lefts):
                first = (k % ratio) * rows
                right = rights[k // ratio][first : first + rows, span]
                term = dot_outer(left[:, part], right)
                total = term if k == 0 else total + term
            out[part, span] = total.astype(BF16)


def outer_blocks(lefts, rights):
    rows = sum(left.shape[0] for left in lefts)
    wide, cols = lefts[0].shape[1], rights[0].shape[1]
    return whole_call(
        functools.partial(outer_kernel, len(lefts)), like(wide, cols, BF16), (*lefts, *rights),
        2 * rows * wide * cols, 2 * rows * (wide + cols),
    )


def cut_kernel(me, gate, up, out):
    @pl.when(pl.program_id(0) == 0)
    def _():
        out[...] = gate[...]

    @pl.when(pl.program_id(0) == 1)
    def _():
        out[...] = up[...]


def cut_columns(me, gate, up, planes, size):
    shard, ff = gate.shape
    mine = ff // planes // size
    if mine % LANES:
        cut = [
            lax.dynamic_slice_in_dim(w.reshape(shard, planes, size, mine), me, 1, 2)
            for w in (gate, up)
        ]
        return jnp.concatenate([c.reshape(shard, planes * mine) for c in cut], axis=1)
    block = pl.BlockSpec((shard, mine), lambda g, z, me_ref: (0, z * size + me_ref[0]))
    return pl.pallas_call(
        cut_kernel,
        out_shape=like(shard, 2 * planes * mine, BF16),
        grid_spec=pltpu.PrefetchScalarGridSpec(
            num_scalar_prefetch=1,
            grid=(2, planes),
            in_specs=[block, block],
            out_specs=pl.BlockSpec((shard, mine), lambda g, z, me_ref: (0, g * planes + z)),
        ),
        name="cut",
    )(me.reshape(1).astype(jnp.int32), gate, up)


def spread_kernel(order, *refs):
    size = (len(refs) - 2) // 2
    gate, up = refs[-2:]
    for r in range(size):
        cols = pl.ds(pl.multiple_of(order[r] * LANES, LANES), LANES)
        gate[:, cols] = refs[r][...].astype(F32)
        up[:, cols] = refs[size + r][...].astype(F32)


def spread_columns(begun, shape, planes, size, order):
    shard, both = shape
    mine = both // 2 // planes
    ff = both // 2 * size
    if size != 8 or mine != LANES:
        pieces = lax.all_gather(begun, "ctx", axis=0)
        wide = pieces.reshape(size, shard, 2, planes, mine).transpose(2, 1, 3, 0, 4)
        wide = wide.reshape(2, shard, ff).astype(F32)
        return wide[0], wide[1]
    pieces = [part for pair in gather_end(begun, size) for part in pair]
    out = pl.BlockSpec((shard, size * mine), lambda z, order_ref: (0, z))
    gate_in = pl.BlockSpec((shard, mine), lambda z, order_ref: (0, z))
    up_in = pl.BlockSpec((shard, mine), lambda z, order_ref: (0, planes + z))
    return pl.pallas_call(
        spread_kernel,
        out_shape=(like(shard, ff, F32), like(shard, ff, F32)),
        grid_spec=pltpu.PrefetchScalarGridSpec(
            num_scalar_prefetch=1,
            grid=(planes,),
            in_specs=[gate_in] * size + [up_in] * size,
            out_specs=(out, out),
        ),
        name="spread",
    )(order, *pieces, *pieces)


def compact_matrix(rows, cols, place):
    source = lax.broadcasted_iota(jnp.int32, (rows, cols), 0)
    target = lax.broadcasted_iota(jnp.int32, (rows, cols), 1)
    return (source == place(target)).astype(BF16)


def heads_kernel(heads, shares, pieces, query, key, value, out):
    size = pieces.shape[0]
    shard = query.shape[0]
    group = LANES * 3

    def select(parts):
        width = pieces.shape[2]
        source = lax.broadcasted_iota(jnp.int32, (width, group), 0)
        target = lax.broadcasted_iota(jnp.int32, (width, group), 1)
        total = None
        for slot, (device, start, span) in enumerate(parts):
            inside = (target >= slot * span) & (target < (slot + 1) * span)
            choose = (inside & (source == target - slot * span + start)).astype(BF16)
            part = dot(pieces[device, :shard, :], choose)
            total = part if total is None else total + part
        return total

    q_cols = heads * HEAD_WIDTH
    per = group // q_cols
    for j in range(size // per):
        parts = [(j * per + i, 0, q_cols) for i in range(per)]
        query[:, j * group : (j + 1) * group] = select(parts)
    per = group // HEAD_WIDTH
    for target, start in ((key, q_cols), (value, q_cols + HEAD_WIDTH)):
        for j in range(KEY_VALUE_HEADS // per):
            parts = [((j * per + i) * shares, start, HEAD_WIDTH) for i in range(per)]
            target[:, j * group : (j + 1) * group] = select(parts)
    rows = pieces.shape[1] - shard
    for z in range(size // 2):
        for q in range(2):
            out[q * rows : (q + 1) * rows, z * shard : (z + 1) * shard] = pieces[
                2 * z + q, shard:, :shard
            ].astype(F32)


def spread_heads(pieces, heads, shares, shard):
    kv = KEY_VALUE_HEADS * HEAD_WIDTH
    out = (like(shard, D, F32), like(shard, kv, F32), like(shard, kv, F32), like(shard, D, F32))
    return whole_call(
        functools.partial(heads_kernel, heads, shares), out, (pieces,),
        4 * shard * D * D, 8 * shard * D,
    )


def after(value, *others):
    return lax.optimization_barrier((value, *others))[0]


def hop(value, size, bit):
    return lax.ppermute(value, "ctx", [(i, i ^ bit) for i in range(size)])


def gather_begin(block, size):
    if size != 8:
        return block
    return block, hop(block, size, 2), hop(block, size, 4)


def gather_end(begun, size):
    if size != 8:
        whole = lax.all_gather(begun, "ctx", axis=0, tiled=True)
        return [tuple(jnp.split(part, 2)) for part in jnp.split(whole, CHUNKS)]
    block, across, along = begun
    half = block.shape[0] // 2
    upper = hop(along[:half], size, 2)
    lower = hop(across[half:], size, 4)
    corner = jnp.concatenate([upper, lower])
    return [(part, hop(part, size, 1)) for part in (block, across, along, corner)]


def gather_rows(block, size):
    return gather_end(gather_begin(block, size), size)


def scatter_rows(pairs, size, before_last=(), before_first=()):
    if size != 8:
        whole = jnp.concatenate([part.astype(BF16) for pair in pairs for part in pair])
        total = lax.psum_scatter(whole, "ctx", scatter_dimension=0, tiled=True).astype(F32)
        return total, total

    def fold(k):
        even, odd = pairs[k]
        return even + hop(odd.astype(BF16), size, 1).astype(F32)

    corner, across, along, own = fold(3), fold(1), fold(2), fold(0)
    half = own.shape[0] // 2

    def send(value, bit):
        return hop(value, size, bit).astype(F32)

    firsts = (corner[:half], corner[half:], across[:half], along[half:])
    firsts = tuple(value.astype(BF16) for value in firsts)
    if before_first:
        firsts = lax.optimization_barrier((*firsts, *before_first))[:4]
    for_along = send(firsts[0], 2)
    for_across = send(firsts[1], 4)
    across_top = send(firsts[2], 2)
    along_low = send(firsts[3], 4)
    across_rest = (across[half:] + for_across).astype(BF16)
    along_rest = (along[:half] + for_along).astype(BF16)
    if before_last:
        across_rest, along_rest, *_ = lax.optimization_barrier(
            (across_rest, along_rest, *before_last)
        )
    across_low = send(across_rest, 2)
    along_top = send(along_rest, 4)
    total = jnp.concatenate(
        [own[:half] + across_top + along_top, own[half:] + across_low + along_low]
    )
    return total, along_rest


def swap_planes(value, size, planes):
    moves = []
    for chip in range(size // 2):
        for core in range(2):
            for z in range(planes):
                moves.append(((chip * 2 + core) * planes + z, (z * 2 + core) * planes + chip))
    return lax.ppermute(value, ("ctx", "fsdp"), moves)


def norm_back(residual, scale_rows, gain, upstream):
    weighted = upstream * gain
    row_inner = jnp.mean(weighted * residual, axis=-1, keepdims=True)
    return scale_rows * weighted - residual * (scale_rows * scale_rows * scale_rows) * row_inner


def local(
    size,
    planes,
    tokens,
    cotangent,
    attend_gain,
    w_query,
    w_key,
    w_value,
    w_out,
    feed_gain,
    w_gate,
    w_up,
    w_down,
    lengths,
    deal_table,
):
    me = lax.axis_index("ctx")
    plane = lax.axis_index("fsdp")
    rows_here = tokens.shape[1]
    rows_all = rows_here * size
    heads = QUERY_HEADS // size
    shares = max(1, size // KEY_VALUE_HEADS)
    shard = w_query.shape[0]
    ff = w_gate.shape[1]
    ff_mine = ff // planes // size
    q_cols = heads * HEAD_WIDTH
    key_head = me // shares
    turn_cols = (heads + 1) * LANES
    piece = rows_all // CHUNKS
    rows_half = piece // 2

    turn_mine = q_cols + HEAD_WIDTH
    cut_cols = turn_mine + HEAD_WIDTH
    wide_cols = turn_cols + LANES

    def place(target):
        turned_col = (target // HALF) * (LANES // 2) + lax.rem(target, HALF)
        return jnp.where(target < turn_mine, turned_col, target - turn_mine + turn_cols)

    compact = compact_matrix(wide_cols, cut_cols, place)
    query_cut = lax.dynamic_slice_in_dim(w_query, me * q_cols, q_cols, 1)
    key_cut = lax.dynamic_slice_in_dim(w_key, key_head * HEAD_WIDTH, HEAD_WIDTH, 1)
    value_cut = lax.dynamic_slice_in_dim(w_value, key_head * HEAD_WIDTH, HEAD_WIDTH, 1)
    gains = jnp.stack([attend_gain, feed_gain])
    gains = jnp.pad(gains, ((0, 14), (0, cut_cols - shard)))
    proj_cut = jnp.concatenate([query_cut, key_cut, value_cut], axis=1)
    proj_all = lax.all_gather(jnp.concatenate([proj_cut, gains]), "fsdp", axis=0)
    gain_one = proj_all[:, shard, :shard].reshape(1, D).astype(F32)
    gain_two = proj_all[:, shard + 1, :shard].reshape(1, D).astype(F32)
    proj_w = dot_t(proj_all[:, :shard].reshape(D, cut_cols), compact).astype(BF16)
    out_piece = lax.dynamic_slice(
        w_out, (lax.rem(me, 2) * q_cols, (me // 2) * shard), (q_cols, shard)
    )
    out_piece = swap_planes(out_piece, size, planes)
    out_rows = q_cols * shard // D
    down_cut = lax.dynamic_slice_in_dim(w_down, me * ff_mine, ff_mine, 0)
    down_all = lax.all_gather(
        jnp.concatenate([down_cut, out_piece.reshape(out_rows, D)]), "fsdp", axis=0
    )
    down_w = down_all[:, :ff_mine].reshape(planes * ff_mine, D)
    out_w = down_all[:, ff_mine:].reshape(planes, q_cols, shard).transpose(1, 0, 2)
    out_w = out_w.reshape(heads, HEAD_WIDTH, D)
    out_w = jnp.pad(out_w, ((0, 0), (0, LANES - HEAD_WIDTH), (0, 0)))
    out_w = out_w.reshape(heads * LANES, D)
    pair_w = lax.all_gather(cut_columns(me, w_gate, w_up, planes, size), "fsdp", axis=0, tiled=True)
    order = jnp.arange(size, dtype=jnp.int32)
    if size == 8:
        order = jnp.bitwise_xor(order, me)
    table = deal_table.reshape(size, rows_here // BLK)[order].reshape(-1)
    pos_all = (table[:, None] * BLK + jnp.arange(BLK, dtype=jnp.int32)[None, :]).reshape(-1)
    live_all = (pos_all < lengths[0]).astype(F32)[:, None]
    if size == 8:
        live = live_all[:rows_here]
    else:
        live = lax.dynamic_slice_in_dim(live_all, me * rows_here, rows_here)
    frequency = ROPE_BASE ** (-2.0 * jnp.arange(HALF, dtype=F32) / HEAD_WIDTH)
    angles = pos_all.astype(F32)[:, None] * frequency[None, :]
    pad = jnp.zeros((rows_all, LANES // 2 - HALF), F32)
    cosine, sine = jnp.cos(angles), jnp.sin(angles)
    cos_t = jnp.concatenate([cosine, pad, cosine, pad], axis=1)
    sin_t = jnp.concatenate([-sine, pad, sine, pad], axis=1)

    def part_of(array, k):
        return array[k * piece : (k + 1) * piece]

    def project_rows(rows, weight):
        half = rows.shape[0] // 2
        odd = dot(rows[half:], weight).astype(BF16)
        return dot(rows[:half], weight), odd

    token_pairs = gather_rows(tokens[0], size)
    residual = tokens[0].astype(F32)
    scale_one = scale_of(residual)
    attend_low, raws = [], []
    for pair in token_pairs:
        even, odd, raw = project_pair(pair, proj_w, gain_one)
        attend_low += [even, odd]
        raws.append(raw)
    ctx_low, *saved = attend(table, lengths, raws, cos_t, sin_t, heads)
    attend_branch, _ = scatter_rows(
        [project_rows(part_of(ctx_low, k), out_w) for k in range(CHUNKS)], size
    )
    middle = residual + attend_branch

    cot_pairs = gather_rows(after(cotangent[0], token_pairs[1][0], token_pairs[2][0]), size)
    scale_two = scale_of(middle)
    feed_pairs = gather_rows((middle * scale_two * gain_two).astype(BF16), size)
    back_low, hidden, pair_back, sums_in = [], [], [], []
    for k in range(CHUNKS):
        low_even, low_odd, hidden_k, pair_k, sum_even, sum_odd = feed_pair(
            feed_pairs[k], cot_pairs[k], part_of(live_all, k), pair_w, down_w
        )
        back_low += [low_even, low_odd]
        hidden.append(hidden_k)
        pair_back.append(pair_k)
        sums_in.append((sum_even, sum_odd))
    pair_grad = outer_blocks([block for pair in feed_pairs for block in pair], pair_back)
    down_grad = outer_blocks(
        [h[i * rows_half : (i + 1) * rows_half] for h in hidden for i in range(2)], back_low,
    )
    back_feed_in, _ = scatter_rows(sums_in, size, (pair_grad, down_grad))
    pair_grad = lax.psum_scatter(pair_grad, "fsdp", scatter_dimension=0, tiled=True)
    down_grad = lax.psum_scatter(down_grad, "fsdp", scatter_dimension=0, tiled=True)
    back_final = cotangent[0].astype(F32) * live
    back_middle = back_final + norm_back(middle, scale_two, gain_two, back_feed_in)
    gain_two_grad = jnp.sum(back_feed_in * middle * scale_two, axis=0)

    mid_pairs = gather_rows(back_middle.astype(BF16), size)
    mid_blocks = [block for pair in mid_pairs for block in pair]
    grad_down = lax.all_gather(
        after(down_grad, mid_blocks[-1]), "ctx", axis=0, tiled=True
    ).astype(F32)
    pair_begun = gather_begin(after(pair_grad, mid_blocks[-1]), size)
    back_context = [dot_t(block, out_w).astype(BF16) for block in mid_blocks]
    turned = attend_back(table, lengths, saved, back_context, cos_t, sin_t, heads)
    if shares > 1:
        pairs = [[g * shares + i for i in range(shares)] for g in range(size // shares)]
        both = lax.psum(turned[:, heads * LANES :].astype(F32), "ctx", axis_index_groups=pairs)
        first = (lax.rem(me, shares) == 0).astype(F32)
        turned = jnp.concatenate([turned[:, : heads * LANES], (both * first).astype(BF16)], axis=1)
    sums_in, gain_sums = [], []
    for k in range(CHUNKS):
        sum_even, sum_odd, gain_sum = project_back_pair(
            part_of(turned, k), proj_w, token_pairs[k]
        )
        sums_in.append((sum_even, sum_odd))
        gain_sums.append(gain_sum)
    sums_in = lax.optimization_barrier(sums_in)
    back_attend_in, attend_sent = scatter_rows(sums_in, size)
    pair_begun = jax.tree.map(lambda value: after(value, attend_sent), pair_begun)
    grad_gate, grad_up = spread_columns(pair_begun, pair_grad.shape, planes, size, order)
    grad_tokens = back_middle + norm_back(residual, scale_one, gain_one, back_attend_in)
    gain_one_grad = (gain_sums[0] + gain_sums[1] + gain_sums[2] + gain_sums[3])[0]

    narrow = dot(turned, compact).astype(BF16)
    proj_grad = outer_blocks(attend_low, [narrow])
    late_ctx = after(ctx_low, turned)
    out_grad = outer_blocks(
        [late_ctx[i * rows_half : (i + 1) * rows_half] for i in range(2 * CHUNKS)], mid_blocks,
    )
    out_grad = out_grad.reshape(heads, LANES, planes, shard)[:, :HEAD_WIDTH]
    out_grad = out_grad.reshape(q_cols, planes, shard).transpose(1, 0, 2)
    out_grad = jnp.pad(out_grad, ((0, 0), (0, 0), (0, cut_cols - shard)))
    head_grad = jnp.concatenate([proj_grad.reshape(planes, shard, cut_cols), out_grad], axis=1)
    head_grad = lax.psum_scatter(head_grad, "fsdp", scatter_dimension=0, tiled=True)[0]
    head_grad = after(head_grad, attend_sent)
    out_piece = swap_planes(head_grad[shard:], size, planes)
    head_grad = lax.all_gather(
        jnp.concatenate([head_grad[:shard], out_piece]), "ctx", axis=0
    )
    grad_query, grad_key, grad_value, grad_out = spread_heads(head_grad, heads, shares, shard)

    parts = [project_rows(after(h, back_middle), down_w) for h in hidden]
    feed_branch, _ = scatter_rows(parts, size, (), (turned,))
    final_sum = middle + feed_branch
    layer_out = (final_sum * live).astype(BF16)
    sums = jnp.stack(
        [
            jnp.sum(final_sum * final_sum * live),
            jnp.sum(attend_branch * attend_branch * live),
            jnp.sum(feed_branch * feed_branch * live),
        ]
    )

    slot = (jnp.arange(planes) == plane).astype(F32)
    stats = jnp.pad(slot[:, None] * sums[None, :], ((0, 0), (0, LANES - 3))).reshape(-1)
    small = after(jnp.concatenate([gain_one_grad, gain_two_grad, stats]), attend_sent)
    if size == 8 and planes == 4:
        for bit in (1, 2, 4):
            small = small + hop(small, size, bit)
        for bit in (1, 2):
            small = small + lax.ppermute(small, "fsdp", [(z, z ^ bit) for z in range(planes)])
    else:
        small = lax.psum(small, ("ctx", "fsdp"))
    grad_attend_gain = lax.dynamic_slice_in_dim(small[:D], plane * shard, shard)
    grad_feed_gain = lax.dynamic_slice_in_dim(small[D : 2 * D], plane * shard, shard)
    total_sums = lax.dynamic_slice_in_dim(small[2 * D :].reshape(planes, LANES), plane, 1)[:, :3]
    rms_stats = jnp.sqrt(total_sums / (lengths.astype(F32)[:, None] * D))
    return (
        layer_out[None],
        grad_tokens[None],
        grad_attend_gain,
        grad_query,
        grad_key,
        grad_value,
        grad_out,
        grad_feed_gain,
        grad_gate,
        grad_up,
        grad_down,
        rms_stats,
    )


def solution(mesh):
    rows = P("fsdp", "ctx", None)
    vector = P("fsdp")
    matrix = P("fsdp", None)
    in_specs = (rows, rows, vector, matrix, matrix, matrix, matrix, vector, matrix, matrix, matrix)
    in_specs += (vector, P())
    out_specs = (rows, rows, vector, matrix, matrix, matrix, matrix, vector, matrix, matrix, matrix)
    out_specs += (matrix,)
    body = functools.partial(local, mesh.shape["ctx"], mesh.shape["fsdp"])


    return jax.shard_map(body, mesh=mesh, in_specs=in_specs, out_specs=out_specs, check_vma=False)
```

profile of v0, /device:TPU:0, one launch (start us, length us, event | category | flops | bytes accessed | tf_op | source)
XLA Modules:
  0.0 664.1 jit_solution(1955175537015291328)
XLA Ops:
  13.7 2.8 collective-permute-start.8
  18.5 19.3 %collective-permute-start.3 = (bf16[256,1536]{1,0:T(8,128)(2,1)S(1)}, bf16[256,1536]{1,0:T(8,128)(2,1)}, u32[]{:S(2)}, u32[]{:S(2)}) collective-permute-start(bf16[256,1536]{1,0:T(8,128)(2,1)S(1)} %bitcast.90), channel_id=1, source_target_pairs={{0,16},{4,20},{8,24},{12,28},{16,0},{20,4},{24,8},{28,12},{1,17},{... | collective-permute-start | bytes 2359304 | tf_op jit(solution)/shard_map/ppermute | solution.py:519
  37.9 3.0 collective-permute-start.1
  40.9 5.3 cut.1
  47.7 3.7 fusion.31
  51.5 2.6 pad_maximum_fusion.4
  57.7 9.0 %collective-permute-done.5 = bf16[128,1536]{1,0:T(8,128)(2,1)S(1)} collective-permute-done((bf16[128,1536]{1,0:T(8,128)(2,1)S(1)}, bf16[128,1536]{1,0:T(8,128)(2,1)S(1)}, u32[]{:S(2)}, u32[]{:S(2)}) %collective-permute-start.5) | collective-permute-done | bytes 393248 | tf_op jit(solution)/shard_map/ppermute | solution.py:519
  68.8 15.3 %collective-permute-done.32.cot_even = bf16[256,1536]{1,0:T(8,128)(2,1)} collective-permute-done((bf16[256,1536]{1,0:T(8,128)(2,1)}, bf16[256,1536]{1,0:T(8,128)(2,1)}, u32[]{:S(2)}, u32[]{:S(2)}) %collective-permute-start.32) | collective-permute-done | bytes 786464 | tf_op jit(solution)/shard_map/ppermute | solution.py:519
  89.7 2.3 shard_map.220
  93.8 2.3 shard_map.221
  98.0 2.6 shard_map.222
  103.3 2.6 shard_map.223
  108.7 36.9 %attend.1 = (bf16[2048,256]{1,0:T(8,128)(2,1)S(1)}, bf16[2,2048,128]{2,1,0:T(8,128)(2,1)S(1)}, bf16[2048,128]{1,0:T(8,128)(2,1)S(1)}, bf16[2048,128]{1,0:T(8,128...) custom-call(s32[16]{0:T(128)S(1)} %reshape.429.table, s32[1]{0:T(128)} %copy.50.length_ref, ...), custom_call_target="tpu_custom_call" | custom-call | flops 2147483648 | bytes 16777216 | tf_op jit(solution)/shard_map/attend/pallas_call | solution.py:131
  151.0 2.2 reshape.432
  153.2 2.3 copy.34
  155.6 2.2 reshape.433
  170.5 5.6 collective-permute-done.14
  178.7 10.4 %collective-permute-done.16 = bf16[128,1536]{1,0:T(8,128)(2,1)S(1)} collective-permute-done((bf16[128,1536]{1,0:T(8,128)(2,1)S(1)}, bf16[128,1536]{1,0:T(8,128)(2,1)S(1)}, u32[]{:S(2)}, u32[]{:S(2)}) %collective-permute-start.16) | collective-permute-done | bytes 393248 | tf_op jit(solution)/shard_map/ppermute | solution.py:519
  196.5 5.7 collective-permute-done.17
  210.7 8.3 %collective-permute-done.24.cot_even = bf16[256,1536]{1,0:T(8,128)(2,1)} collective-permute-done((bf16[256,1536]{1,0:T(8,128)(2,1)}, bf16[256,1536]{1,0:T(8,128)(2,1)}, u32[]{:S(2)}, u32[]{:S(2)}) %collective-permute-start.24) | collective-permute-done | bytes 786464 | tf_op jit(solution)/shard_map/ppermute | solution.py:519
  224.9 2.6 collective-permute-done.33
  231.7 4.8 collective-permute-done.34
  247.0 9.1 %shard_map.224 = (bf16[256,1536]{1,0:T(8,128)(2,1)S(1)}, bf16[256,1536]{1,0:T(8,128)(2,1)S(1)}, bf16[512,512]{1,0:T(8,128)(2,1)S(1)}, bf16[512,1024]{1,0:T(8,128...) custom-call(bf16[256,1536]{1,0:T(8,128)(2,1)} %multiply_convert_fusion.feed_even.refs_0_, ...), custom_call_target="tpu_custom_call" | custom-call | flops 4026531840 | bytes 7864320 | tf_op jit(solution)/shard_map/pallas_call | solution.py:263
  261.1 9.6 %shard_map.225 = (bf16[256,1536]{1,0:T(8,128)(2,1)S(1)}, bf16[256,1536]{1,0:T(8,128)(2,1)S(1)}, bf16[512,512]{1,0:T(8,128)(2,1)S(1)}, bf16[512,1024]{1,0:T(8,128...) custom-call(bf16[256,1536]{1,0:T(8,128)(2,1)} %collective-permute-done.22.feed_even.refs_2_, ...), custom_call_target="tpu_custom_call" | custom-call | flops 4026531840 | bytes 7864320 | tf_op jit(solution)/shard_map/pallas_call | solution.py:263
  272.9 8.9 %shard_map.227 = (bf16[256,1536]{1,0:T(8,128)(2,1)S(1)}, bf16[256,1536]{1,0:T(8,128)(2,1)S(1)}, bf16[512,512]{1,0:T(8,128)(2,1)S(1)}, bf16[512,1024]{1,0:T(8,128...) custom-call(bf16[256,1536]{1,0:T(8,128)(2,1)} %collective-permute-done.28.feed_even.refs_4_, ...), custom_call_target="tpu_custom_call" | custom-call | flops 4026531840 | bytes 7864320 | tf_op jit(solution)/shard_map/pallas_call | solution.py:263
  284.9 9.0 %shard_map.226 = (bf16[256,1536]{1,0:T(8,128)(2,1)S(1)}, bf16[256,1536]{1,0:T(8,128)(2,1)S(1)}, bf16[512,512]{1,0:T(8,128)(2,1)S(1)}, bf16[512,1024]{1,0:T(8,128...) custom-call(bf16[256,1536]{1,0:T(8,128)(2,1)S(1)} %constant_dynamic-update-slice_fusion.2.feed_even.refs_6_, ...), custom_call_target="tpu_custom_call" | custom-call | flops 4026531840 | bytes 7864320 | tf_op jit(solution)/shard_map/pallas_call | solution.py:263
  296.9 13.1 %shard_map.228 = bf16[1536,1024]{1,0:T(8,128)(2,1)} custom-call(bf16[256,1536]{1,0:T(8,128)(2,1)} %multiply_convert_fusion.feed_even.refs_0_, bf16[256,1536]{1,0:T(8,128)(2,1)} %collective-permute-done.19.feed_odd.refs_1_, bf16[256,1536]{1,0:T(8,128)(2,1)} %collective-permute-done.22.feed_even.refs_2_, ...), custom_call_target="tpu_custom_call" | custom-call | flops 6442450944 | bytes 10485760 | tf_op jit(solution)/shard_map/pallas_call | solution.py:263
  322.3 6.4 shard_map.229
  339.2 6.1 collective-permute-done.37
  346.2 5.1 collective-permute-done.41
  352.7 2.5 convert_add_fusion.10
  355.5 7.2 %collective-permute-done.42 = bf16[128,1536]{1,0:T(8,128)(2,1)} collective-permute-done((bf16[128,1536]{1,0:T(8,128)(2,1)}, bf16[128,1536]{1,0:T(8,128)(2,1)}, u32[]{:S(2)}, u32[]{:S(2)}) %collective-permute-start.42) | collective-permute-done | bytes 393248 | tf_op jit(solution)/shard_map/ppermute | solution.py:519
  362.8 2.1 fusion.24
  371.9 13.4 %collective-permute-done.52.refs_12_ = bf16[256,1536]{1,0:T(8,128)(2,1)S(1)} collective-permute-done((bf16[256,1536]{1,0:T(8,128)(2,1)S(1)}, bf16[256,1536]{1,0:T(8,128)(2,1)S(1)}, u32[]{:S(2)}, u32[]{:S(2)}) %collective-permute-start.52) | collective-permute-done | bytes 786464 | tf_op jit(solution)/shard_map/ppermute | solution.py:519
  389.2 5.7 collective-permute-done.54
  398.2 35.4 %attend_back.1 = bf16[2048,512]{1,0:T(8,128)(2,1)} custom-call(s32[16]{0:T(128)S(1)} %reshape.429.table, s32[1]{0:T(128)} %copy.50.length_ref, bf16[2,2048,128]{2,1,0:T(8,128)(2,1)S(1)} %copy-done.56, bf16[2048,128]{1,0:T(8,128)(2,1)S(1)} %copy-done.71, bf16[2048,128]{1,0:T(8,128)(2,1)S(1)} %copy-done.73, f32[2048,256]{1,0:T(8,128)} %get-tuple-element.138.ctx_s, ...), custom_call_target="tpu_custom_call" | custom-call | flops 5368709120 | bytes 16777216 | tf_op jit(solution)/shard_map/attend_back/pallas_call | solution.py:240
  433.6 3.4 shard_map.235
  437.9 2.4 reshape.439
  441.7 4.2 convolution_convert_fusion.1.refs_8_
  445.9 7.2 %shard_map.234 = bf16[1536,384]{1,0:T(8,128)(2,1)} custom-call(bf16[256,1536]{1,0:T(8,128)(2,1)S(1)} %copy-done.24, bf16[256,1536]{1,0:T(8,128)(2,1)S(1)} %copy-done.26, bf16[256,1536]{1,0:T(8,128)(2,1)S(1)} %copy-done.28, bf16[256,1536]{1,0:T(8,128)(2,1)S(1)} %copy-done.30, bf16[256,1536]{1,0:T(8,128)(2,1)S(1)} %copy-done.32, ...), custom_call_target="tpu_custom_call" | custom-call | flops 2415919104 | bytes 7864320 | tf_op jit(solution)/shard_map/pallas_call | solution.py:263
  453.1 2.7 pad_maximum_fusion
  456.7 3.1 convolution_convert_fusion.6
  465.4 2.4 convert_add_fusion.5
  478.1 2.5 shard_map.233
  480.6 2.5 shard_map.232
  483.1 2.8 shard_map.231
  487.1 2.2 shard_map.230
  489.4 2.1 fusion.19
  496.7 9.3 %collective-permute-done.68 = bf16[128,1536]{1,0:T(8,128)(2,1)S(1)} collective-permute-done((bf16[128,1536]{1,0:T(8,128)(2,1)S(1)}, bf16[128,1536]{1,0:T(8,128)(2,1)S(1)}, u32[]{:S(2)}, u32[]{:S(2)}) %collective-permute-start.68) | collective-permute-done | bytes 393248 | tf_op jit(solution)/shard_map/ppermute | solution.py:519
  510.4 3.4 convert_add_fusion.7
  523.9 22.0 %collective-permute-start.74 = (f32[3584]{0:T(1024)S(1)}, f32[3584]{0:T(1024)S(1)}, u32[]{:S(2)}, u32[]{:S(2)}) collective-permute-start(f32[3584]{0:T(1024)S(1)} %add.340), channel_id=1, source_target_pairs={{0,8},{4,12},{8,0},{12,4},{16,24},{20,28},{24,16},{28,20},{1,9},{5... | collective-permute-start | bytes 43016 | tf_op jit(solution)/shard_map/ppermute | solution.py:519
  556.0 2.5 convert_add_fusion.4
  560.5 2.3 collective-permute-start.77
  562.8 11.7 %collective-permute-done.70 = bf16[128,1536]{1,0:T(8,128)(2,1)S(1)} collective-permute-done((bf16[128,1536]{1,0:T(8,128)(2,1)S(1)}, bf16[128,1536]{1,0:T(8,128)(2,1)S(1)}, u32[]{:S(2)}, u32[]{:S(2)}) %collective-permute-start.70) | collective-permute-done | bytes 393248 | tf_op jit(solution)/shard_map/ppermute | solution.py:519
  582.4 4.4 collective-permute-done.69
  586.8 4.9 collective-permute-done.71
  593.0 18.1 %collective-permute-done.82.refs_4_.refs_12_ = bf16[384,1024]{1,0:T(8,128)(2,1)S(1)} collective-permute-done((bf16[384,1024]{1,0:T(8,128)(2,1)}, bf16[384,1024]{1,0:T(8,128)(2,1)S(1)}, u32[]{:S(2)}, u32[]{:S(2)}) %collective-permute-start.82) | collective-permute-done | bytes 786464 | tf_op jit(solution)/shard_map/ppermute | solution.py:519
  611.0 4.4 collective-permute-done.80.refs_2_.refs_10_
  618.5 4.9 collective-permute-done.84
  624.1 2.1 fusion.2
  628.2 9.0 %spread.1 = (f32[384,4096]{1,0:T(8,128)}, f32[384,4096]{1,0:T(8,128)}) custom-call(s32[8]{0:T(128)} %iota_xor_fusion.order, bf16[384,1024]{1,0:T(8,128)(2,1)} %reduce-scatter.6.cloned.1.call-done.refs_0_.refs_8_, bf16[384,1024]{1,0:T(8,128)(2,1)} %copy-done.103, bf16[384,1024]{1,0:T(8,128)(2,1)} %copy-done.98, bf16[384,1024]{1,0:T(8,128)(2,1)} %copy-done.104, ...), custom_call_target="tpu_custom_call" | custom-call | tf_op jit(solution)/shard_map/spread/pallas_call | solution.py:451
  637.3 5.5 convert_element_type.382
  642.8 6.2 all-gather.17.cloned.1.call-done
  651.0 5.8 shard_map.236
  (590 shorter events, 207.4 us)
Async XLA Ops:
  7.2 78.7 %all-gather.13.cloned.1.call-start = ((), (), s32[]{:S(2)}) async-start(), calls=%async_computation.8 | async-start | bytes 1536000 | tf_op jit(solution)/shard_map/all_gather | solution.py:644
  12.0 137.1 %all-gather.15.cloned.1.call-start = ((), (), s32[]{:S(2)}) async-start(), calls=%async_computation.9 | async-start | bytes 2703360 | tf_op jit(solution)/shard_map/all_gather | solution.py:654
  18.5 227.5 %all-gather.9.cloned.1.call-start = ((), (), s32[]{:S(2)}) async-start(), calls=%async_computation.3 | async-start | bytes 3932160 | tf_op jit(solution)/shard_map/all_gather | solution.py:662
  18.5 35.6 %collective-permute-start.3 = (bf16[256,1536]{1,0:T(8,128)(2,1)S(1)}, bf16[256,1536]{1,0:T(8,128)(2,1)}, u32[]{:S(2)}, u32[]{:S(2)}) collective-permute-start(bf16[256,1536]{1,0:T(8,128)(2,1)S(1)} %bitcast.90), channel_id=1, source_target_pairs={{0,16},{4,20},{8,24},{12,28},{16,0},{20,4},{24,8},{28,12},{1,17},{... | collective-permute-start | bytes 2359304 | tf_op jit(solution)/shard_map/ppermute | solution.py:519
  37.9 17.5 %collective-permute-start.1 = (bf16[256,1536]{1,0:T(8,128)(2,1)S(1)}, bf16[256,1536]{1,0:T(8,128)(2,1)S(1)}, u32[]{:S(2)}, u32[]{:S(2)}) collective-permute-start(bf16[256,1536]{1,0:T(8,128)(2,1)S(1)} %bitcast.91), channel_id=1, source_target_pairs={{0,8},{4,12},{8,0},{12,4},{16,24},{20,28},{24,16},{28,20},{1,9},{5... | collective-permute-start | bytes 2359304 | tf_op jit(solution)/shard_map/ppermute | solution.py:519
  40.8 48.8 %collective-permute-start = (bf16[256,1536]{1,0:T(8,128)(2,1)S(1)}, bf16[256,1536]{1,0:T(8,128)(2,1)}, u32[]{:S(2)}, u32[]{:S(2)}) collective-permute-start(bf16[256,1536]{1,0:T(8,128)(2,1)S(1)} %bitcast.92), channel_id=1, source_target_pairs={{0,4},{4,0},{8,12},{12,8},{16,20},{20,16},{24,28},{28,24},{1,5},{5... | collective-permute-start | bytes 2359304 | tf_op jit(solution)/shard_map/ppermute | solution.py:519
  46.2 419.1 %reduce-scatter.8.cloned.1.call-start = ((), (), s32[]{:S(2)}) async-start(), calls=%async_computation.6 | async-start | bytes 1966080 | tf_op jit(solution)/shard_map/reduce_scatter | solution.py:720
  55.4 12.1 %collective-permute-start.6 = (bf16[128,1536]{1,0:T(8,128)(2,1)S(1)}, bf16[128,1536]{1,0:T(8,128)(2,1)S(1)}, u32[]{:S(2)}, u32[]{:S(2)}) collective-permute-start(bf16[128,1536]{1,0:T(8,128)(2,1)S(1)} %slice.453), channel_id=1, source_target_pairs={{0,16},{4,20},{8,24},{12,28},{16,0},{20,4},{24,8},{28,12},{1,17},{... | collective-permute-start | bytes 1179656 | tf_op jit(solution)/shard_map/ppermute | solution.py:519
  57.3 26.7 %collective-permute-start.32 = (bf16[256,1536]{1,0:T(8,128)(2,1)}, bf16[256,1536]{1,0:T(8,128)(2,1)}, u32[]{:S(2)}, u32[]{:S(2)}) collective-permute-start(bf16[256,1536]{1,0:T(8,128)(2,1)} %bitcast.10.cot_even), channel_id=1, source_target_pairs={{0,16},{4,20},{8,24},{12,28},{16,0},{20,4},{24,8},{28,12},{1,17},{... | collective-permute-start | bytes 2359304 | tf_op jit(solution)/shard_map/ppermute | solution.py:519
  57.5 40.5 %collective-permute-start.4 = (bf16[256,1536]{1,0:T(8,128)(2,1)}, bf16[256,1536]{1,0:T(8,128)(2,1)}, u32[]{:S(2)}, u32[]{:S(2)}) collective-permute-start(bf16[256,1536]{1,0:T(8,128)(2,1)} %collective-permute-done.3.even), channel_id=1, source_target_pairs={{0,4},{4,0},{8,12},{12,8},{16,20},{20,16},{24,28},{28,24},{1,5},{5... | collective-permute-start | bytes 2359304 | tf_op jit(solution)/shard_map/ppermute | solution.py:519
  66.7 27.1 %collective-permute-start.2 = (bf16[256,1536]{1,0:T(8,128)(2,1)S(1)}, bf16[256,1536]{1,0:T(8,128)(2,1)}, u32[]{:S(2)}, u32[]{:S(2)}) collective-permute-start(bf16[256,1536]{1,0:T(8,128)(2,1)S(1)} %collective-permute-done.1.even), channel_id=1, source_target_pairs={{0,4},{4,0},{8,12},{12,8},{16,20},{20,16},{24,28},{28,24},{1,5},{5... | collective-permute-start | bytes 2359304 | tf_op jit(solution)/shard_map/ppermute | solution.py:519
  68.3 35.1 %collective-permute-start.7 = (bf16[256,1536]{1,0:T(8,128)(2,1)}, bf16[256,1536]{1,0:T(8,128)(2,1)}, u32[]{:S(2)}, u32[]{:S(2)}) collective-permute-start(bf16[256,1536]{1,0:T(8,128)(2,1)} %constant_dynamic-update-slice_fusion.even), channel_id=1, source_target_pairs={{0,4},{4,0},{8,12},{12,8},{16,20},{20,16},{24,28},{28,24},{1,5},{5... | collective-permute-start | bytes 2359304 | tf_op jit(solution)/shard_map/ppermute | solution.py:519
  163.1 29.3 %collective-permute-start.9 = (bf16[256,1536]{1,0:T(8,128)(2,1)}, bf16[256,1536]{1,0:T(8,128)(2,1)}, u32[]{:S(2)}, u32[]{:S(2)}) collective-permute-start(bf16[256,1536]{1,0:T(8,128)(2,1)} %convolution_convert_fusion.5), channel_id=1, source_target_pairs={{0,4},{4,0},{8,12},{12,8},{16,20},{20,16},{24,28},{28,24},{1,5},{5... | collective-permute-start | bytes 2359304 | tf_op jit(solution)/shard_map/ppermute | solution.py:519
  167.0 27.6 %collective-permute-start.11 = (bf16[128,1536]{1,0:T(8,128)(2,1)}, bf16[128,1536]{1,0:T(8,128)(2,1)}, u32[]{:S(2)}, u32[]{:S(2)}) collective-permute-start(bf16[128,1536]{1,0:T(8,128)(2,1)} %slice.639), channel_id=1, source_target_pairs={{0,8},{4,12},{8,0},{12,4},{16,24},{20,28},{24,16},{28,20},{1,9},{5... | collective-permute-start | bytes 1179656 | tf_op jit(solution)/shard_map/ppermute | solution.py:519
  168.5 26.2 %collective-permute-start.18 = (bf16[128,1536]{1,0:T(8,128)(2,1)}, bf16[128,1536]{1,0:T(8,128)(2,1)}, u32[]{:S(2)}, u32[]{:S(2)}) collective-permute-start(bf16[128,1536]{1,0:T(8,128)(2,1)} %slice.638), channel_id=1, source_target_pairs={{0,16},{4,20},{8,24},{12,28},{16,0},{20,4},{24,8},{28,12},{1,17},{... | collective-permute-start | bytes 1179656 | tf_op jit(solution)/shard_map/ppermute | solution.py:519
  170.2 18.9 %collective-permute-start.16 = (bf16[128,1536]{1,0:T(8,128)(2,1)S(1)}, bf16[128,1536]{1,0:T(8,128)(2,1)S(1)}, u32[]{:S(2)}, u32[]{:S(2)}) collective-permute-start(bf16[128,1536]{1,0:T(8,128)(2,1)S(1)} %get-tuple-element.226), channel_id=1, source_target_pairs={{0,16},{4,20},{8,24},{12,28},{16,0},{20,4},{24,8},{28,12},{1,17},{... | collective-permute-start | bytes 1179656 | tf_op jit(solution)/shard_map/ppermute | solution.py:519
  176.9 19.6 %collective-permute-start.15 = (bf16[128,1536]{1,0:T(8,128)(2,1)}, bf16[128,1536]{1,0:T(8,128)(2,1)}, u32[]{:S(2)}, u32[]{:S(2)}) collective-permute-start(bf16[128,1536]{1,0:T(8,128)(2,1)} %fusion.27), channel_id=1, source_target_pairs={{0,16},{4,20},{8,24},{12,28},{16,0},{20,4},{24,8},{28,12},{1,17},{... | collective-permute-start | bytes 1179656 | tf_op jit(solution)/shard_map/ppermute | solution.py:519
  189.9 12.3 %collective-permute-start.17 = (bf16[128,1536]{1,0:T(8,128)(2,1)}, bf16[128,1536]{1,0:T(8,128)(2,1)}, u32[]{:S(2)}, u32[]{:S(2)}) collective-permute-start(bf16[128,1536]{1,0:T(8,128)(2,1)} %fusion.25), channel_id=1, source_target_pairs={{0,8},{4,12},{8,0},{12,4},{16,24},{20,28},{24,16},{28,20},{1,9},{5... | collective-permute-start | bytes 1179656 | tf_op jit(solution)/shard_map/ppermute | solution.py:519
  192.4 26.6 %collective-permute-start.24 = (bf16[256,1536]{1,0:T(8,128)(2,1)}, bf16[256,1536]{1,0:T(8,128)(2,1)}, u32[]{:S(2)}, u32[]{:S(2)}) collective-permute-start(bf16[256,1536]{1,0:T(8,128)(2,1)} %bitcast.10.cot_even), channel_id=1, source_target_pairs={{0,8},{4,12},{8,0},{12,4},{16,24},{20,28},{24,16},{28,20},{1,9},{5... | collective-permute-start | bytes 2359304 | tf_op jit(solution)/shard_map/ppermute | solution.py:519
  194.6 49.7 %collective-permute-start.20 = (bf16[256,1536]{1,0:T(8,128)(2,1)}, bf16[256,1536]{1,0:T(8,128)(2,1)}, u32[]{:S(2)}, u32[]{:S(2)}) collective-permute-start(bf16[256,1536]{1,0:T(8,128)(2,1)} %bitcast.10.cot_even), channel_id=1, source_target_pairs={{0,4},{4,0},{8,12},{12,8},{16,20},{20,16},{24,28},{28,24},{1,5},{5... | collective-permute-start | bytes 2359304 | tf_op jit(solution)/shard_map/ppermute | solution.py:519
  194.7 32.8 %collective-permute-start.33 = (bf16[128,1536]{1,0:T(8,128)(2,1)}, bf16[128,1536]{1,0:T(8,128)(2,1)}, u32[]{:S(2)}, u32[]{:S(2)}) collective-permute-start(bf16[128,1536]{1,0:T(8,128)(2,1)} %slice.473), channel_id=1, source_target_pairs={{0,8},{4,12},{8,0},{12,4},{16,24},{20,28},{24,16},{28,20},{1,9},{5... | collective-permute-start | bytes 1179656 | tf_op jit(solution)/shard_map/ppermute | solution.py:519
  207.3 31.3 %collective-permute-start.28 = (bf16[256,1536]{1,0:T(8,128)(2,1)}, bf16[256,1536]{1,0:T(8,128)(2,1)}, u32[]{:S(2)}, u32[]{:S(2)}) collective-permute-start(bf16[256,1536]{1,0:T(8,128)(2,1)} %multiply_convert_fusion.feed_even.refs_0_), channel_id=1, source_target_pairs={{0,16},{4,20},{8,24},{12,28},{16,0},{20,4},{24,8},{28,12},{1,17},{... | collective-permute-start | bytes 2359304 | tf_op jit(solution)/shard_map/ppermute | solution.py:519
  209.0 31.8 %collective-permute-start.22 = (bf16[256,1536]{1,0:T(8,128)(2,1)}, bf16[256,1536]{1,0:T(8,128)(2,1)}, u32[]{:S(2)}, u32[]{:S(2)}) collective-permute-start(bf16[256,1536]{1,0:T(8,128)(2,1)} %multiply_convert_fusion.feed_even.refs_0_), channel_id=1, source_target_pairs={{0,8},{4,12},{8,0},{12,4},{16,24},{20,28},{24,16},{28,20},{1,9},{5... | collective-permute-start | bytes 2359304 | tf_op jit(solution)/shard_map/ppermute | solution.py:519
  219.1 27.0 %collective-permute-start.19 = (bf16[256,1536]{1,0:T(8,128)(2,1)}, bf16[256,1536]{1,0:T(8,128)(2,1)}, u32[]{:S(2)}, u32[]{:S(2)}) collective-permute-start(bf16[256,1536]{1,0:T(8,128)(2,1)} %multiply_convert_fusion.feed_even.refs_0_), channel_id=1, source_target_pairs={{0,4},{4,0},{8,12},{12,8},{16,20},{20,16},{24,28},{28,24},{1,5},{5... | collective-permute-start | bytes 2359304 | tf_op jit(solution)/shard_map/ppermute | solution.py:519
  236.5 35.9 %collective-permute-start.39 = (bf16[256,1536]{1,0:T(8,128)(2,1)}, bf16[256,1536]{1,0:T(8,128)(2,1)}, u32[]{:S(2)}, u32[]{:S(2)}) collective-permute-start(bf16[256,1536]{1,0:T(8,128)(2,1)} %collective-permute-done.32.cot_even), channel_id=1, source_target_pairs={{0,4},{4,0},{8,12},{12,8},{16,20},{20,16},{24,28},{28,24},{1,5},{5... | collective-permute-start | bytes 2359304 | tf_op jit(solution)/shard_map/ppermute | solution.py:519
  238.5 21.8 %collective-permute-start.25 = (bf16[256,1536]{1,0:T(8,128)(2,1)}, bf16[256,1536]{1,0:T(8,128)(2,1)}, u32[]{:S(2)}, u32[]{:S(2)}) collective-permute-start(bf16[256,1536]{1,0:T(8,128)(2,1)} %collective-permute-done.24.cot_even), channel_id=1, source_target_pairs={{0,4},{4,0},{8,12},{12,8},{16,20},{20,16},{24,28},{28,24},{1,5},{5... | collective-permute-start | bytes 2359304 | tf_op jit(solution)/shard_map/ppermute | solution.py:519
  240.8 16.9 %collective-permute-start.29 = (bf16[128,1536]{1,0:T(8,128)(2,1)}, bf16[128,1536]{1,0:T(8,128)(2,1)}, u32[]{:S(2)}, u32[]{:S(2)}) collective-permute-start(bf16[128,1536]{1,0:T(8,128)(2,1)} %slice.471), channel_id=1, source_target_pairs={{0,8},{4,12},{8,0},{12,4},{16,24},{20,28},{24,16},{28,20},{1,9},{5... | collective-permute-start | bytes 1179656 | tf_op jit(solution)/shard_map/ppermute | solution.py:519
  244.3 14.9 %collective-permute-start.30 = (bf16[128,1536]{1,0:T(8,128)(2,1)}, bf16[128,1536]{1,0:T(8,128)(2,1)}, u32[]{:S(2)}, u32[]{:S(2)}) collective-permute-start(bf16[128,1536]{1,0:T(8,128)(2,1)} %slice.472), channel_id=1, source_target_pairs={{0,16},{4,20},{8,24},{12,28},{16,0},{20,4},{24,8},{28,12},{1,17},{... | collective-permute-start | bytes 1179656 | tf_op jit(solution)/shard_map/ppermute | solution.py:519
  246.0 14.9 %collective-permute-start.23 = (bf16[256,1536]{1,0:T(8,128)(2,1)}, bf16[256,1536]{1,0:T(8,128)(2,1)}, u32[]{:S(2)}, u32[]{:S(2)}) collective-permute-start(bf16[256,1536]{1,0:T(8,128)(2,1)} %collective-permute-done.22.feed_even.refs_2_), channel_id=1, source_target_pairs={{0,4},{4,0},{8,12},{12,8},{16,20},{20,16},{24,28},{28,24},{1,5},{5... | collective-permute-start | bytes 2359304 | tf_op jit(solution)/shard_map/ppermute | solution.py:519
  257.7 15.2 %collective-permute-start.38 = (bf16[256,1536]{1,0:T(8,128)(2,1)}, bf16[256,1536]{1,0:T(8,128)(2,1)S(1)}, u32[]{:S(2)}, u32[]{:S(2)}) collective-permute-start(bf16[256,1536]{1,0:T(8,128)(2,1)} %collective-permute-done.28.feed_even.refs_4_), channel_id=1, source_target_pairs={{0,4},{4,0},{8,12},{12,8},{16,20},{20,16},{24,28},{28,24},{1,5},{5... | collective-permute-start | bytes 2359304 | tf_op jit(solution)/shard_map/ppermute | solution.py:519
  259.3 24.7 %collective-permute-start.35 = (bf16[256,1536]{1,0:T(8,128)(2,1)}, bf16[256,1536]{1,0:T(8,128)(2,1)S(1)}, u32[]{:S(2)}, u32[]{:S(2)}) collective-permute-start(bf16[256,1536]{1,0:T(8,128)(2,1)} %constant_dynamic-update-slice_fusion.4.cot_even), channel_id=1, source_target_pairs={{0,4},{4,0},{8,12},{12,8},{16,20},{20,16},{24,28},{28,24},{1,5},{5... | collective-permute-start | bytes 2359304 | tf_op jit(solution)/shard_map/ppermute | solution.py:519
  260.4 92.3 %collective-permute-start.21 = (bf16[256,1536]{1,0:T(8,128)(2,1)}, bf16[256,1536]{1,0:T(8,128)(2,1)}, u32[]{:S(2)}, u32[]{:S(2)}) collective-permute-start(bf16[256,1536]{1,0:T(8,128)(2,1)} %get-tuple-element.107), channel_id=1, source_target_pairs={{0,4},{4,0},{8,12},{12,8},{16,20},{20,16},{24,28},{28,24},{1,5},{5... | collective-permute-start | bytes 2359304 | tf_op jit(solution)/shard_map/ppermute | solution.py:519
  261.0 23.1 %collective-permute-start.31 = (bf16[256,1536]{1,0:T(8,128)(2,1)S(1)}, bf16[256,1536]{1,0:T(8,128)(2,1)S(1)}, u32[]{:S(2)}, u32[]{:S(2)}) collective-permute-start(bf16[256,1536]{1,0:T(8,128)(2,1)S(1)} %constant_dynamic-update-slice_fusion.2.feed_even.refs_6_), channel_id=1, source_target_pairs={{0,4},{4,0},{8,12},{12,8},{16,20},{20,16},{24,28},{28,24},{1,5},{5... | collective-permute-start | bytes 2359304 | tf_op jit(solution)/shard_map/ppermute | solution.py:519
  272.5 56.3 %collective-permute-start.26 = (bf16[256,1536]{1,0:T(8,128)(2,1)}, bf16[256,1536]{1,0:T(8,128)(2,1)}, u32[]{:S(2)}, u32[]{:S(2)}) collective-permute-start(bf16[256,1536]{1,0:T(8,128)(2,1)} %get-tuple-element.109), channel_id=1, source_target_pairs={{0,4},{4,0},{8,12},{12,8},{16,20},{20,16},{24,28},{28,24},{1,5},{5... | collective-permute-start | bytes 2359304 | tf_op jit(solution)/shard_map/ppermute | solution.py:519
  281.9 51.8 %collective-permute-start.40 = (bf16[256,1536]{1,0:T(8,128)(2,1)}, bf16[256,1536]{1,0:T(8,128)(2,1)}, u32[]{:S(2)}, u32[]{:S(2)}) collective-permute-start(bf16[256,1536]{1,0:T(8,128)(2,1)} %get-tuple-element.113), channel_id=1, source_target_pairs={{0,4},{4,0},{8,12},{12,8},{16,20},{20,16},{24,28},{28,24},{1,5},{5... | collective-permute-start | bytes 2359304 | tf_op jit(solution)/shard_map/ppermute | solution.py:519
  296.5 35.4 %collective-permute-start.36 = (bf16[256,1536]{1,0:T(8,128)(2,1)}, bf16[256,1536]{1,0:T(8,128)(2,1)}, u32[]{:S(2)}, u32[]{:S(2)}) collective-permute-start(bf16[256,1536]{1,0:T(8,128)(2,1)} %get-tuple-element.111), channel_id=1, source_target_pairs={{0,4},{4,0},{8,12},{12,8},{16,20},{20,16},{24,28},{28,24},{1,5},{5... | collective-permute-start | bytes 2359304 | tf_op jit(solution)/shard_map/ppermute | solution.py:519
  331.5 24.0 %collective-permute-start.27 = (bf16[128,1536]{1,0:T(8,128)(2,1)}, bf16[128,1536]{1,0:T(8,128)(2,1)}, u32[]{:S(2)}, u32[]{:S(2)}) collective-permute-start(bf16[128,1536]{1,0:T(8,128)(2,1)} %slice.637), channel_id=1, source_target_pairs={{0,8},{4,12},{8,0},{12,4},{16,24},{20,28},{24,16},{28,20},{1,9},{5... | collective-permute-start | bytes 1179656 | tf_op jit(solution)/shard_map/ppermute | solution.py:519
  333.3 12.1 %collective-permute-start.37 = (bf16[128,1536]{1,0:T(8,128)(2,1)S(1)}, bf16[128,1536]{1,0:T(8,128)(2,1)S(1)}, u32[]{:S(2)}, u32[]{:S(2)}) collective-permute-start(bf16[128,1536]{1,0:T(8,128)(2,1)S(1)} %get-tuple-element.224), channel_id=1, source_target_pairs={{0,16},{4,20},{8,24},{12,28},{16,0},{20,4},{24,8},{28,12},{1,17},{... | collective-permute-start | bytes 1179656 | tf_op jit(solution)/shard_map/ppermute | solution.py:519
  336.8 18.7 %collective-permute-start.44 = (bf16[128,1536]{1,0:T(8,128)(2,1)}, bf16[128,1536]{1,0:T(8,128)(2,1)}, u32[]{:S(2)}, u32[]{:S(2)}) collective-permute-start(bf16[128,1536]{1,0:T(8,128)(2,1)} %slice.636), channel_id=1, source_target_pairs={{0,16},{4,20},{8,24},{12,28},{16,0},{20,4},{24,8},{28,12},{1,17},{... | collective-permute-start | bytes 1179656 | tf_op jit(solution)/shard_map/ppermute | solution.py:519
  337.5 13.7 %collective-permute-start.41 = (bf16[128,1536]{1,0:T(8,128)(2,1)S(1)}, bf16[128,1536]{1,0:T(8,128)(2,1)S(1)}, u32[]{:S(2)}, u32[]{:S(2)}) collective-permute-start(bf16[128,1536]{1,0:T(8,128)(2,1)S(1)} %get-tuple-element.223), channel_id=1, source_target_pairs={{0,8},{4,12},{8,0},{12,4},{16,24},{20,28},{24,16},{28,20},{1,9},{5... | collective-permute-start | bytes 1179656 | tf_op jit(solution)/shard_map/ppermute | solution.py:519
  355.3 153.1 %reduce-scatter.4.cloned.1.call-start = ((), (), s32[]{:S(2)}) async-start(), calls=%async_computation.4 | async-start | bytes 2211840 | tf_op jit(solution)/shard_map/reduce_scatter | solution.py:762
  367.4 17.9 %collective-permute-start.52 = (bf16[256,1536]{1,0:T(8,128)(2,1)S(1)}, bf16[256,1536]{1,0:T(8,128)(2,1)S(1)}, u32[]{:S(2)}, u32[]{:S(2)}) collective-permute-start(bf16[256,1536]{1,0:T(8,128)(2,1)S(1)} %subtract_add_fusion.refs_8_), channel_id=1, source_target_pairs={{0,16},{4,20},{8,24},{12,28},{16,0},{20,4},{24,8},{28,12},{1,17},{... | collective-permute-start | bytes 2359304 | tf_op jit(solution)/shard_map/ppermute | solution.py:519
  369.1 18.1 %collective-permute-start.50 = (bf16[256,1536]{1,0:T(8,128)(2,1)S(1)}, bf16[256,1536]{1,0:T(8,128)(2,1)S(1)}, u32[]{:S(2)}, u32[]{:S(2)}) collective-permute-start(bf16[256,1536]{1,0:T(8,128)(2,1)S(1)} %subtract_add_fusion.refs_8_), channel_id=1, source_target_pairs={{0,8},{4,12},{8,0},{12,4},{16,24},{20,28},{24,16},{28,20},{1,9},{5... | collective-permute-start | bytes 2359304 | tf_op jit(solution)/shard_map/ppermute | solution.py:519
  369.7 19.1 %collective-permute-start.49 = (bf16[256,1536]{1,0:T(8,128)(2,1)S(1)}, bf16[256,1536]{1,0:T(8,128)(2,1)S(1)}, u32[]{:S(2)}, u32[]{:S(2)}) collective-permute-start(bf16[256,1536]{1,0:T(8,128)(2,1)S(1)} %subtract_add_fusion.refs_8_), channel_id=1, source_target_pairs={{0,4},{4,0},{8,12},{12,8},{16,20},{20,16},{24,28},{28,24},{1,5},{5... | collective-permute-start | bytes 2359304 | tf_op jit(solution)/shard_map/ppermute | solution.py:519
  455.8 121.4 %reduce-scatter.6.cloned.1.call-start = ((), (), s32[]{:S(2)}) async-start(), calls=%async_computation.5 | async-start | bytes 3932160 | tf_op jit(solution)/shard_map/reduce_scatter | solution.py:719
  456.4 180.9 %all-gather.11.cloned.1.call-start = ((), (), s32[]{:S(2)}) async-start(), calls=%async_computation.7 | async-start | bytes 3538944 | tf_op jit(solution)/shard_map/all_gather | solution.py:727
  465.3 44.1 %collective-permute-start.45 = (bf16[256,1536]{1,0:T(8,128)(2,1)}, bf16[256,1536]{1,0:T(8,128)(2,1)}, u32[]{:S(2)}, u32[]{:S(2)}) collective-permute-start(bf16[256,1536]{1,0:T(8,128)(2,1)} %convolution_convert_fusion.9), channel_id=1, source_target_pairs={{0,4},{4,0},{8,12},{12,8},{16,20},{20,16},{24,28},{28,24},{1,5},{5... | collective-permute-start | bytes 2359304 | tf_op jit(solution)/shard_map/ppermute | solution.py:519
  465.3 183.7 %all-gather.17.cloned.1.call-start = ((), (), s32[]{:S(2)}) async-start(), calls=%async_computation.10 | async-start | bytes 3981312 | tf_op jit(solution)/shard_map/all_gather | solution.py:765
  473.9 15.4 %collective-permute-start.58 = (bf16[128,1536]{1,0:T(8,128)(2,1)S(1)}, bf16[128,1536]{1,0:T(8,128)(2,1)}, u32[]{:S(2)}, u32[]{:S(2)}) collective-permute-start(bf16[128,1536]{1,0:T(8,128)(2,1)S(1)} %get-tuple-element.141), channel_id=1, source_target_pairs={{0,8},{4,12},{8,0},{12,4},{16,24},{20,28},{24,16},{28,20},{1,9},{5... | collective-permute-start | bytes 1179656 | tf_op jit(solution)/shard_map/ppermute | solution.py:519
  474.8 40.0 %collective-permute-start.57 = (bf16[128,1536]{1,0:T(8,128)(2,1)}, bf16[128,1536]{1,0:T(8,128)(2,1)}, u32[]{:S(2)}, u32[]{:S(2)}) collective-permute-start(bf16[128,1536]{1,0:T(8,128)(2,1)} %slice.635), channel_id=1, source_target_pairs={{0,8},{4,12},{8,0},{12,4},{16,24},{20,28},{24,16},{28,20},{1,9},{5... | collective-permute-start | bytes 1179656 | tf_op jit(solution)/shard_map/ppermute | solution.py:519
  476.1 15.4 %collective-permute-start.60 = (bf16[128,1536]{1,0:T(8,128)(2,1)}, bf16[128,1536]{1,0:T(8,128)(2,1)}, u32[]{:S(2)}, u32[]{:S(2)}) collective-permute-start(bf16[128,1536]{1,0:T(8,128)(2,1)} %get-tuple-element.142), channel_id=1, source_target_pairs={{0,16},{4,20},{8,24},{12,28},{16,0},{20,4},{24,8},{28,12},{1,17},{... | collective-permute-start | bytes 1179656 | tf_op jit(solution)/shard_map/ppermute | solution.py:519
  476.5 38.9 %collective-permute-start.62 = (bf16[128,1536]{1,0:T(8,128)(2,1)}, bf16[128,1536]{1,0:T(8,128)(2,1)}, u32[]{:S(2)}, u32[]{:S(2)}) collective-permute-start(bf16[128,1536]{1,0:T(8,128)(2,1)} %slice.634), channel_id=1, source_target_pairs={{0,16},{4,20},{8,24},{12,28},{16,0},{20,4},{24,8},{28,12},{1,17},{... | collective-permute-start | bytes 1179656 | tf_op jit(solution)/shard_map/ppermute | solution.py:519
  493.6 21.8 %collective-permute-start.59 = (bf16[128,1536]{1,0:T(8,128)(2,1)}, bf16[128,1536]{1,0:T(8,128)(2,1)}, u32[]{:S(2)}, u32[]{:S(2)}) collective-permute-start(bf16[128,1536]{1,0:T(8,128)(2,1)} %fusion.19), channel_id=1, source_target_pairs={{0,16},{4,20},{8,24},{12,28},{16,0},{20,4},{24,8},{28,12},{1,17},{... | collective-permute-start | bytes 1179656 | tf_op jit(solution)/shard_map/ppermute | solution.py:519
  513.8 42.1 %collective-permute-start.63 = (bf16[256,1536]{1,0:T(8,128)(2,1)S(1)}, bf16[256,1536]{1,0:T(8,128)(2,1)}, u32[]{:S(2)}, u32[]{:S(2)}) collective-permute-start(bf16[256,1536]{1,0:T(8,128)(2,1)S(1)} %copy-done.53), channel_id=1, source_target_pairs={{0,4},{4,0},{8,12},{12,8},{16,20},{20,16},{24,28},{28,24},{1,5},{5... | collective-permute-start | bytes 2359304 | tf_op jit(solution)/shard_map/ppermute | solution.py:519
  514.8 32.8 %collective-permute-start.64 = (bf16[256,1536]{1,0:T(8,128)(2,1)}, bf16[256,1536]{1,0:T(8,128)(2,1)}, u32[]{:S(2)}, u32[]{:S(2)}) collective-permute-start(bf16[256,1536]{1,0:T(8,128)(2,1)} %get-tuple-element.155), channel_id=1, source_target_pairs={{0,4},{4,0},{8,12},{12,8},{16,20},{20,16},{24,28},{28,24},{1,5},{5... | collective-permute-start | bytes 2359304 | tf_op jit(solution)/shard_map/ppermute | solution.py:519
  523.9 23.7 %collective-permute-start.74 = (f32[3584]{0:T(1024)S(1)}, f32[3584]{0:T(1024)S(1)}, u32[]{:S(2)}, u32[]{:S(2)}) collective-permute-start(f32[3584]{0:T(1024)S(1)} %add.340), channel_id=1, source_target_pairs={{0,8},{4,12},{8,0},{12,4},{16,24},{20,28},{24,16},{28,20},{1,9},{5... | collective-permute-start | bytes 43016 | tf_op jit(solution)/shard_map/ppermute | solution.py:519
  551.9 27.3 %collective-permute-start.65 = (bf16[128,1536]{1,0:T(8,128)(2,1)}, bf16[128,1536]{1,0:T(8,128)(2,1)S(1)}, u32[]{:S(2)}, u32[]{:S(2)}) collective-permute-start(bf16[128,1536]{1,0:T(8,128)(2,1)} %slice.633), channel_id=1, source_target_pairs={{0,8},{4,12},{8,0},{12,4},{16,24},{20,28},{24,16},{28,20},{1,9},{5... | collective-permute-start | bytes 1179656 | tf_op jit(solution)/shard_map/ppermute | solution.py:519
  553.9 28.5 %collective-permute-start.72 = (bf16[128,1536]{1,0:T(8,128)(2,1)}, bf16[128,1536]{1,0:T(8,128)(2,1)}, u32[]{:S(2)}, u32[]{:S(2)}) collective-permute-start(bf16[128,1536]{1,0:T(8,128)(2,1)} %slice.632), channel_id=1, source_target_pairs={{0,16},{4,20},{8,24},{12,28},{16,0},{20,4},{24,8},{28,12},{1,17},{... | collective-permute-start | bytes 1179656 | tf_op jit(solution)/shard_map/ppermute | solution.py:519
  555.9 18.6 %collective-permute-start.70 = (bf16[128,1536]{1,0:T(8,128)(2,1)S(1)}, bf16[128,1536]{1,0:T(8,128)(2,1)S(1)}, u32[]{:S(2)}, u32[]{:S(2)}) collective-permute-start(bf16[128,1536]{1,0:T(8,128)(2,1)S(1)} %copy-done.114), channel_id=1, source_target_pairs={{0,16},{4,20},{8,24},{12,28},{16,0},{20,4},{24,8},{28,12},{1,17},{... | collective-permute-start | bytes 1179656 | tf_op jit(solution)/shard_map/ppermute | solution.py:519
  558.5 28.3 %collective-permute-start.69 = (bf16[128,1536]{1,0:T(8,128)(2,1)}, bf16[128,1536]{1,0:T(8,128)(2,1)S(1)}, u32[]{:S(2)}, u32[]{:S(2)}) collective-permute-start(bf16[128,1536]{1,0:T(8,128)(2,1)} %fusion.15), channel_id=1, source_target_pairs={{0,16},{4,20},{8,24},{12,28},{16,0},{20,4},{24,8},{28,12},{1,17},{... | collective-permute-start | bytes 1179656 | tf_op jit(solution)/shard_map/ppermute | solution.py:519
  560.5 14.8 %collective-permute-start.77 = (f32[3584]{0:T(1024)S(1)}, f32[3584]{0:T(1024)S(1)}, u32[]{:S(2)}, u32[]{:S(2)}) collective-permute-start(f32[3584]{0:T(1024)S(1)} %add.343), channel_id=1, source_target_pairs={{0,2},{1,3},{2,0},{3,1},{4,6},{5,7},{6,4},{7,5},{8,10},{9,11},{10,... | collective-permute-start | bytes 43016 | tf_op jit(solution)/shard_map/ppermute | solution.py:789
  575.3 16.4 %collective-permute-start.71 = (bf16[128,1536]{1,0:T(8,128)(2,1)}, bf16[128,1536]{1,0:T(8,128)(2,1)S(1)}, u32[]{:S(2)}, u32[]{:S(2)}) collective-permute-start(bf16[128,1536]{1,0:T(8,128)(2,1)} %fusion.13), channel_id=1, source_target_pairs={{0,8},{4,12},{8,0},{12,4},{16,24},{20,28},{24,16},{28,20},{1,9},{5... | collective-permute-start | bytes 1179656 | tf_op jit(solution)/shard_map/ppermute | solution.py:519
  577.2 33.9 %collective-permute-start.82 = (bf16[384,1024]{1,0:T(8,128)(2,1)}, bf16[384,1024]{1,0:T(8,128)(2,1)S(1)}, u32[]{:S(2)}, u32[]{:S(2)}) collective-permute-start(bf16[384,1024]{1,0:T(8,128)(2,1)} %reduce-scatter.6.cloned.1.call-done.refs_0_.refs_8_), channel_id=1, source_target_pairs={{0,16},{4,20},{8,24},{12,28},{16,0},{20,4},{24,8},{28,12},{1,17},{... | collective-permute-start | bytes 2359304 | tf_op jit(solution)/shard_map/ppermute | solution.py:519
  579.2 36.3 %collective-permute-start.80 = (bf16[384,1024]{1,0:T(8,128)(2,1)}, bf16[384,1024]{1,0:T(8,128)(2,1)S(1)}, u32[]{:S(2)}, u32[]{:S(2)}) collective-permute-start(bf16[384,1024]{1,0:T(8,128)(2,1)} %reduce-scatter.6.cloned.1.call-done.refs_0_.refs_8_), channel_id=1, source_target_pairs={{0,8},{4,12},{8,0},{12,4},{16,24},{20,28},{24,16},{28,20},{1,9},{5... | collective-permute-start | bytes 2359304 | tf_op jit(solution)/shard_map/ppermute | solution.py:519
  (166 other events, 1155.3 us)
Sparse Core Ops, SparseCore 0:
  12.1 38.0 all-gather.12
  52.3 47.0 all-gather.14
  101.5 62.2 all-gather.8
  355.4 36.8 reduce-scatter.7
  455.9 39.7 reduce-scatter.3
  498.4 68.9 reduce-scatter.5
  569.3 43.5 all-gather.10
  614.8 34.1 all-gather.16
where the time goes:
time: 676 us; the launch traced here: 664 us
  Pallas kernels  179 us (26%)
  waiting for transfers between devices  171 us (25%)
  starting transfers between devices  106 us (16%)
  local copies, waits for them, and re-layouts  99.4 us (15%)
  other arithmetic  59.6 us (9%)
  matrix products  31.6 us (5%)
  between operations  17.1 us (3%)
    ppermute x83, waiting for transfers between devices, hop(): return lax.ppermute(value, 'ctx', [(i, i ^ bit) for i in range(size)])  164 us
    ppermute x83, starting transfers between devices, hop(): return lax.ppermute(value, 'ctx', [(i, i ^ bit) for i in range(size)])  99.3 us
    pallas_call x17, Pallas kernels, whole_call(): pl.pallas_call(kernel, out_shape=out_shape, in_specs=[vmem] * len(args),...  92.5 us
    unnamed x274, local copies, waits for them, and re-layouts  43.8 us
    pallas_call x1, Pallas kernels, attend(): pl.pallas_call(functools.partial(attend_kernel, heads), out_shape=(jax.Sh...  36.9 us
    pallas_call x1, Pallas kernels, attend_back(): pl.pallas_call(functools.partial(attend_back_kernel, heads), out_shape=ja...  35.4 us
    dot_general x17, matrix products, dot(): lax.dot_general(left, right, (((1,), (0,)), ((), ())), preferred_element_...  27.3 us
  transfers between devices with their start and end apart: 95, of which 29 were waited for; matrix products, arithmetic and copies ran while one was open for 22% of the time, Pallas kernels for 26%

commit v1 on v0

--- a/solution.py
+++ b/solution.py
@@ -545,7 +545,7 @@
     if size != 8:
         whole = jnp.concatenate([part.astype(BF16) for pair in pairs for part in pair])
         total = lax.psum_scatter(whole, "ctx", scatter_dimension=0, tiled=True).astype(F32)
-        return total, total
+        return total, (total,)
 
     def fold(k):
         even, odd = pairs[k]
@@ -576,7 +576,7 @@
     total = jnp.concatenate(
         [own[:half] + across_top + along_top, own[half:] + across_low + along_low]
     )
-    return total, along_rest
+    return total, (along_rest, across_rest, across_top, along_low)
 
 
 def swap_planes(value, size, planes):
@@ -649,17 +649,18 @@
         w_out, (lax.rem(me, 2) * q_cols, (me // 2) * shard), (q_cols, shard)
     )
     out_piece = swap_planes(out_piece, size, planes)
-    out_rows = q_cols * shard // D
     down_cut = lax.dynamic_slice_in_dim(w_down, me * ff_mine, ff_mine, 0)
-    down_all = lax.all_gather(
-        jnp.concatenate([down_cut, out_piece.reshape(out_rows, D)]), "fsdp", axis=0
-    )
-    down_w = down_all[:, :ff_mine].reshape(planes * ff_mine, D)
-    out_w = down_all[:, ff_mine:].reshape(planes, q_cols, shard).transpose(1, 0, 2)
+    blocks = [down_cut[:, z * shard : (z + 1) * shard] for z in range(planes)]
+    down_all = lax.all_gather(jnp.concatenate([*blocks, out_piece]), "fsdp", axis=0)
+    down_rows = planes * ff_mine
+    down_w = down_all[:, :down_rows].reshape(planes, planes, ff_mine, shard)
+    down_w = down_w.transpose(0, 2, 1, 3).reshape(down_rows, D)
+    out_w = down_all[:, down_rows:].transpose(1, 0, 2).reshape(q_cols, D)
     out_w = out_w.reshape(heads, HEAD_WIDTH, D)
     out_w = jnp.pad(out_w, ((0, 0), (0, LANES - HEAD_WIDTH), (0, 0)))
     out_w = out_w.reshape(heads * LANES, D)
-    pair_w = lax.all_gather(cut_columns(me, w_gate, w_up, planes, size), "fsdp", axis=0, tiled=True)
+    pair_cut = cut_columns(me, w_gate, w_up, planes, size)
+    pair_w = lax.all_gather(pair_cut, "fsdp", axis=0, tiled=True)
     order = jnp.arange(size, dtype=jnp.int32)
     if size == 8:
         order = jnp.bitwise_xor(order, me)
@@ -685,7 +686,10 @@
         odd = dot(rows[half:], weight).astype(BF16)
         return dot(rows[:half], weight), odd
 
-    token_pairs = gather_rows(tokens[0], size)
+    begun = gather_begin(tokens[0], size)
+    if size == 8:
+        begun = (begun[0], *lax.optimization_barrier((*begun[1:], pair_cut))[:2])
+    token_pairs = gather_end(begun, size)
     residual = tokens[0].astype(F32)
     scale_one = scale_of(residual)
     attend_low, raws = [], []
@@ -699,7 +703,7 @@
     )
     middle = residual + attend_branch
 
-    cot_pairs = gather_rows(after(cotangent[0], token_pairs[1][0], token_pairs[2][0]), size)
+    cot_pairs = gather_rows(after(cotangent[0], token_pairs[3][0]), size)
     scale_two = scale_of(middle)
     feed_pairs = gather_rows((middle * scale_two * gain_two).astype(BF16), size)
     back_low, hidden, pair_back, sums_in = [], [], [], []
@@ -743,8 +747,8 @@
         sums_in.append((sum_even, sum_odd))
         gain_sums.append(gain_sum)
     sums_in = lax.optimization_barrier(sums_in)
-    back_attend_in, attend_sent = scatter_rows(sums_in, size)
-    pair_begun = jax.tree.map(lambda value: after(value, attend_sent), pair_begun)
+    back_attend_in, attend_sent = scatter_rows(sums_in, size, (), (turned,))
+    pair_begun = jax.tree.map(lambda value: after(value, *attend_sent), pair_begun)
     grad_gate, grad_up = spread_columns(pair_begun, pair_grad.shape, planes, size, order)
     grad_tokens = back_middle + norm_back(residual, scale_one, gain_one, back_attend_in)
     gain_one_grad = (gain_sums[0] + gain_sums[1] + gain_sums[2] + gain_sums[3])[0]
@@ -760,14 +764,15 @@
     out_grad = jnp.pad(out_grad, ((0, 0), (0, 0), (0, cut_cols - shard)))
     head_grad = jnp.concatenate([proj_grad.reshape(planes, shard, cut_cols), out_grad], axis=1)
     head_grad = lax.psum_scatter(head_grad, "fsdp", scatter_dimension=0, tiled=True)[0]
-    head_grad = after(head_grad, attend_sent)
+    head_grad = after(head_grad, *attend_sent)
     out_piece = swap_planes(head_grad[shard:], size, planes)
     head_grad = lax.all_gather(
         jnp.concatenate([head_grad[:shard], out_piece]), "ctx", axis=0
     )
     grad_query, grad_key, grad_value, grad_out = spread_heads(head_grad, heads, shares, shard)
 
-    parts = [project_rows(after(h, back_middle), down_w) for h in hidden]
+    late = [after(hidden[0], *attend_sent)] + [after(h, back_middle) for h in hidden[1:]]
+    parts = [project_rows(h, down_w) for h in late]
     feed_branch, _ = scatter_rows(parts, size, (), (turned,))
     final_sum = middle + feed_branch
     layer_out = (final_sum * live).astype(BF16)
@@ -781,7 +786,7 @@
 
     slot = (jnp.arange(planes) == plane).astype(F32)
     stats = jnp.pad(slot[:, None] * sums[None, :], ((0, 0), (0, LANES - 3))).reshape(-1)
-    small = after(jnp.concatenate([gain_one_grad, gain_two_grad, stats]), attend_sent)
+    small = after(jnp.concatenate([gain_one_grad, gain_two_grad, stats]), *attend_sent)
     if size == 8 and planes == 4:
         for bit in (1, 2, 4):
             small = small + hop(small, size, bit)

time: 676 us -> 652 us (0.964)
  waiting for transfers between devices: 171 us -> 162 us
    ppermute x83, waiting for transfers between devices: 164 us -> 142 us  [hop(): return lax.ppermute(value, 'ctx', [(i, i ^ bit) for i in range(size)])]
    all_gather x1, waiting for transfers between devices: 6.18 us -> 15.4 us  [local(): lax.all_gather(jnp.concatenate([head_grad[:shard], out_piece]), 'ctx', ax...]
    unnamed x274 -> x279, local copies, waits for them, and re-layouts: 43.8 us -> 48.3 us
  transfers between devices with their start and end apart: 95 -> 95, of which waited for: 29 -> 26; matrix products, arithmetic and copies ran while one was open for 22% -> 21% of each run, Pallas kernels for 26% -> 27%
where the time goes in v1:
time: 652 us; the launch traced here: 641 us
  Pallas kernels  179 us (27%)
  waiting for transfers between devices  162 us (25%)
  starting transfers between devices  101 us (15%)
  local copies, waits for them, and re-layouts  96 us (15%)
  other arithmetic  57.3 us (9%)
  matrix products  27.8 us (4%)
  between operations  17.2 us (3%)
    ppermute x83, waiting for transfers between devices, hop(): return lax.ppermute(value, 'ctx', [(i, i ^ bit) for i in range(size)])  142 us
    ppermute x83, starting transfers between devices, hop(): return lax.ppermute(value, 'ctx', [(i, i ^ bit) for i in range(size)])  99 us
    pallas_call x17, Pallas kernels, whole_call(): pl.pallas_call(kernel, out_shape=out_shape, in_specs=[vmem] * len(args),...  92.4 us
    unnamed x279, local copies, waits for them, and re-layouts  48.3 us
    pallas_call x1, Pallas kernels, attend(): pl.pallas_call(functools.partial(attend_kernel, heads), out_shape=(jax.Sh...  36.4 us
    pallas_call x1, Pallas kernels, attend_back(): pl.pallas_call(functools.partial(attend_back_kernel, heads), out_shape=ja...  35.5 us
    dot_general x17, matrix products, dot(): lax.dot_general(left, right, (((1,), (0,)), ((), ())), preferred_element_...  23.6 us
    all_gather x1, waiting for transfers between devices, local(): lax.all_gather(jnp.concatenate([head_grad[:shard], out_piece]), 'ctx', ax...  15.4 us
  transfers between devices with their start and end apart: 95, of which 26 were waited for; matrix products, arithmetic and copies ran while one was open for 21% of the time, Pallas kernels for 27%

profile of v1, /device:TPU:0, one launch (start us, length us, event | category | flops | bytes accessed | tf_op | source)
XLA Modules:
  0.0 640.6 jit_solution(6111413841398660834)
XLA Ops:
  17.2 14.9 %collective-permute-start.2 = (bf16[256,1536]{1,0:T(8,128)(2,1)S(1)}, bf16[256,1536]{1,0:T(8,128)(2,1)}, u32[]{:S(2)}, u32[]{:S(2)}) collective-permute-start(bf16[256,1536]{1,0:T(8,128)(2,1)S(1)} %bitcast.96), channel_id=1, source_target_pairs={{0,16},{4,20},{8,24},{12,28},{16,0},{20,4},{24,8},{28,12},{1,17},{... | collective-permute-start | bytes 2359304 | tf_op jit(solution)/shard_map/ppermute | solution.py:519
  32.1 6.5 %collective-permute-start.1 = (bf16[256,1536]{1,0:T(8,128)(2,1)S(1)}, bf16[256,1536]{1,0:T(8,128)(2,1)S(1)}, u32[]{:S(2)}, u32[]{:S(2)}) collective-permute-start(bf16[256,1536]{1,0:T(8,128)(2,1)S(1)} %bitcast.97), channel_id=1, source_target_pairs={{0,8},{4,12},{8,0},{12,4},{16,24},{20,28},{24,16},{28,20},{1,9},{5... | collective-permute-start | bytes 2359304 | tf_op jit(solution)/shard_map/ppermute | solution.py:519
  38.7 5.3 cut.1
  45.5 3.7 fusion.31
  49.3 2.5 pad_maximum_fusion.4
  55.7 8.8 %collective-permute-done.5 = bf16[128,1536]{1,0:T(8,128)(2,1)S(1)} collective-permute-done((bf16[128,1536]{1,0:T(8,128)(2,1)S(1)}, bf16[128,1536]{1,0:T(8,128)(2,1)S(1)}, u32[]{:S(2)}, u32[]{:S(2)}) %collective-permute-start.5) | collective-permute-done | bytes 393248 | tf_op jit(solution)/shard_map/ppermute | solution.py:519
  66.1 2.0 collective-permute-start.32
  71.9 2.3 shard_map.220
  76.1 2.6 shard_map.222
  81.4 2.3 shard_map.221
  85.7 2.6 shard_map.223
  91.0 36.4 %attend.1 = (bf16[2048,256]{1,0:T(8,128)(2,1)S(1)}, bf16[2,2048,128]{2,1,0:T(8,128)(2,1)S(1)}, bf16[2048,128]{1,0:T(8,128)(2,1)S(1)}, bf16[2048,128]{1,0:T(8,128...) custom-call(s32[16]{0:T(128)S(1)} %reshape.424.table, s32[1]{0:T(128)} %copy.50.length_ref, ...), custom_call_target="tpu_custom_call" | custom-call | flops 2147483648 | bytes 16777216 | tf_op jit(solution)/shard_map/attend/pallas_call | solution.py:131
  133.3 2.2 reshape_reshape.3
  146.3 7.5 %collective-permute-done.14 = bf16[128,1536]{1,0:T(8,128)(2,1)S(1)} collective-permute-done((bf16[128,1536]{1,0:T(8,128)(2,1)S(1)}, bf16[128,1536]{1,0:T(8,128)(2,1)S(1)}, u32[]{:S(2)}, u32[]{:S(2)}) %collective-permute-start.14) | collective-permute-done | bytes 393248 | tf_op jit(solution)/shard_map/ppermute | solution.py:519
  154.8 10.8 %collective-permute-done.16 = bf16[128,1536]{1,0:T(8,128)(2,1)S(1)} collective-permute-done((bf16[128,1536]{1,0:T(8,128)(2,1)S(1)}, bf16[128,1536]{1,0:T(8,128)(2,1)S(1)}, u32[]{:S(2)}, u32[]{:S(2)}) %collective-permute-start.16) | collective-permute-done | bytes 393248 | tf_op jit(solution)/shard_map/ppermute | solution.py:519
  175.7 3.3 collective-permute-done.17
  186.9 9.0 %collective-permute-done.24.cot_even = bf16[256,1536]{1,0:T(8,128)(2,1)} collective-permute-done((bf16[256,1536]{1,0:T(8,128)(2,1)}, bf16[256,1536]{1,0:T(8,128)(2,1)}, u32[]{:S(2)}, u32[]{:S(2)}) %collective-permute-start.24) | collective-permute-done | bytes 786464 | tf_op jit(solution)/shard_map/ppermute | solution.py:519
  201.7 2.6 collective-permute-done.33
  208.4 4.9 collective-permute-done.34
  224.7 9.1 %shard_map.224 = (bf16[256,1536]{1,0:T(8,128)(2,1)S(1)}, bf16[256,1536]{1,0:T(8,128)(2,1)S(1)}, bf16[512,512]{1,0:T(8,128)(2,1)S(1)}, bf16[512,1024]{1,0:T(8,128...) custom-call(bf16[256,1536]{1,0:T(8,128)(2,1)} %multiply_convert_fusion.feed_even.refs_0_, ...), custom_call_target="tpu_custom_call" | custom-call | flops 4026531840 | bytes 7864320 | tf_op jit(solution)/shard_map/pallas_call | solution.py:263
  238.8 9.6 %shard_map.225 = (bf16[256,1536]{1,0:T(8,128)(2,1)S(1)}, bf16[256,1536]{1,0:T(8,128)(2,1)S(1)}, bf16[512,512]{1,0:T(8,128)(2,1)S(1)}, bf16[512,1024]{1,0:T(8,128...) custom-call(bf16[256,1536]{1,0:T(8,128)(2,1)} %collective-permute-done.22.feed_even.refs_2_, ...), custom_call_target="tpu_custom_call" | custom-call | flops 4026531840 | bytes 7864320 | tf_op jit(solution)/shard_map/pallas_call | solution.py:263
  250.6 8.9 %shard_map.227 = (bf16[256,1536]{1,0:T(8,128)(2,1)S(1)}, bf16[256,1536]{1,0:T(8,128)(2,1)S(1)}, bf16[512,512]{1,0:T(8,128)(2,1)S(1)}, bf16[512,1024]{1,0:T(8,128...) custom-call(bf16[256,1536]{1,0:T(8,128)(2,1)} %collective-permute-done.28.feed_even.refs_4_, ...), custom_call_target="tpu_custom_call" | custom-call | flops 4026531840 | bytes 7864320 | tf_op jit(solution)/shard_map/pallas_call | solution.py:263
  262.6 9.0 %shard_map.226 = (bf16[256,1536]{1,0:T(8,128)(2,1)S(1)}, bf16[256,1536]{1,0:T(8,128)(2,1)S(1)}, bf16[512,512]{1,0:T(8,128)(2,1)S(1)}, bf16[512,1024]{1,0:T(8,128...) custom-call(bf16[256,1536]{1,0:T(8,128)(2,1)S(1)} %constant_dynamic-update-slice_fusion.3.feed_even.refs_6_, ...), custom_call_target="tpu_custom_call" | custom-call | flops 4026531840 | bytes 7864320 | tf_op jit(solution)/shard_map/pallas_call | solution.py:263
  274.5 13.1 %shard_map.228 = bf16[1536,1024]{1,0:T(8,128)(2,1)} custom-call(bf16[256,1536]{1,0:T(8,128)(2,1)} %multiply_convert_fusion.feed_even.refs_0_, bf16[256,1536]{1,0:T(8,128)(2,1)} %collective-permute-done.19.feed_odd.refs_1_, bf16[256,1536]{1,0:T(8,128)(2,1)} %collective-permute-done.22.feed_even.refs_2_, ...), custom_call_target="tpu_custom_call" | custom-call | flops 6442450944 | bytes 10485760 | tf_op jit(solution)/shard_map/pallas_call | solution.py:263
  299.9 6.8 %shard_map.229 = bf16[512,1536]{1,0:T(8,128)(2,1)} custom-call(bf16[256,512]{1,0:T(8,128)(2,1)S(1)} %copy-done.40, bf16[256,512]{1,0:T(8,128)(2,1)S(1)} %copy-done.39, bf16[256,512]{1,0:T(8,128)(2,1)S(1)} %copy-done.42, bf16[256,512]{1,0:T(8,128)(2,1)S(1)} %copy-done.41, bf16[256,512]{1,0:T(8,128)(2,1)S(1)} %copy-done.44, bf16[256,512]{1,0:T(8,128)(2,1)S(1)} %copy-done.43, ...), custom_call_target="tpu_custom_call" | custom-call | flops 3221225472 | bytes 8388608 | tf_op jit(solution)/shard_map/pallas_call | solution.py:263
  317.2 6.7 %collective-permute-done.37 = bf16[128,1536]{1,0:T(8,128)(2,1)S(1)} collective-permute-done((bf16[128,1536]{1,0:T(8,128)(2,1)S(1)}, bf16[128,1536]{1,0:T(8,128)(2,1)S(1)}, u32[]{:S(2)}, u32[]{:S(2)}) %collective-permute-start.37) | collective-permute-done | bytes 393248 | tf_op jit(solution)/shard_map/ppermute | solution.py:519
  324.7 4.6 collective-permute-done.41
  331.3 2.5 convert_add_fusion.10
  333.9 6.9 %collective-permute-done.42 = bf16[128,1536]{1,0:T(8,128)(2,1)} collective-permute-done((bf16[128,1536]{1,0:T(8,128)(2,1)}, bf16[128,1536]{1,0:T(8,128)(2,1)}, u32[]{:S(2)}, u32[]{:S(2)}) %collective-permute-start.42) | collective-permute-done | bytes 393248 | tf_op jit(solution)/shard_map/ppermute | solution.py:519
  340.9 2.1 fusion.24
  350.9 13.3 %collective-permute-done.48.refs_12_ = bf16[256,1536]{1,0:T(8,128)(2,1)S(1)} collective-permute-done((bf16[256,1536]{1,0:T(8,128)(2,1)S(1)}, bf16[256,1536]{1,0:T(8,128)(2,1)S(1)}, u32[]{:S(2)}, u32[]{:S(2)}) %collective-permute-start.48) | collective-permute-done | bytes 786464 | tf_op jit(solution)/shard_map/ppermute | solution.py:519
  368.6 5.3 collective-permute-done.50
  377.1 35.5 %attend_back.1 = bf16[2048,512]{1,0:T(8,128)(2,1)} custom-call(s32[16]{0:T(128)S(1)} %reshape.424.table, s32[1]{0:T(128)} %copy.50.length_ref, bf16[2,2048,128]{2,1,0:T(8,128)(2,1)S(1)} %copy-done.54, bf16[2048,128]{1,0:T(8,128)(2,1)S(1)} %copy-done.69, bf16[2048,128]{1,0:T(8,128)(2,1)S(1)} %copy-done.71, f32[2048,256]{1,0:T(8,128)} %get-tuple-element.117.ctx_s, ...), custom_call_target="tpu_custom_call" | custom-call | flops 5368709120 | bytes 16777216 | tf_op jit(solution)/shard_map/attend_back/pallas_call | solution.py:240
  412.7 3.4 shard_map.235
  417.1 2.4 reshape.432
  420.8 4.2 convolution_convert_fusion.1.refs_8_
  425.0 7.2 %shard_map.234 = bf16[1536,384]{1,0:T(8,128)(2,1)} custom-call(bf16[256,1536]{1,0:T(8,128)(2,1)S(1)} %copy-done.22, bf16[256,1536]{1,0:T(8,128)(2,1)S(1)} %copy-done.24, bf16[256,1536]{1,0:T(8,128)(2,1)S(1)} %copy-done.30, bf16[256,1536]{1,0:T(8,128)(2,1)S(1)} %copy-done.32, bf16[256,1536]{1,0:T(8,128)(2,1)S(1)} %copy-done.26, ...), custom_call_target="tpu_custom_call" | custom-call | flops 2415919104 | bytes 7864320 | tf_op jit(solution)/shard_map/pallas_call | solution.py:263
  432.2 2.7 pad_maximum_fusion
  436.1 3.0 convolution_convert_fusion.6
  445.1 2.5 shard_map.233
  447.6 2.5 shard_map.232
  450.1 2.2 shard_map.231
  452.3 2.4 shard_map.230
  454.9 2.5 convert_add_fusion.3
  471.7 5.9 collective-permute-done.56
  478.4 2.1 collective-permute-done.57
  481.3 12.5 %collective-permute-done.58 = bf16[128,1536]{1,0:T(8,128)(2,1)S(1)} collective-permute-done((bf16[128,1536]{1,0:T(8,128)(2,1)S(1)}, bf16[128,1536]{1,0:T(8,128)(2,1)S(1)}, u32[]{:S(2)}, u32[]{:S(2)}) %collective-permute-start.58) | collective-permute-done | bytes 393248 | tf_op jit(solution)/shard_map/ppermute | solution.py:519
  496.4 2.4 collective-permute-start.64
  498.7 3.9 collective-permute-start.67
  506.2 14.8 %collective-permute-start.66 = (bf16[128,1536]{1,0:T(8,128)(2,1)S(1)}, bf16[128,1536]{1,0:T(8,128)(2,1)S(1)}, u32[]{:S(2)}, u32[]{:S(2)}) collective-permute-start(bf16[128,1536]{1,0:T(8,128)(2,1)S(1)} %fusion.17), channel_id=1, source_target_pairs={{0,16},{4,20},{8,24},{12,28},{16,0},{20,4},{24,8},{28,12},{1,17},{... | collective-permute-start | bytes 1179656 | tf_op jit(solution)/shard_map/ppermute | solution.py:519
  522.9 6.9 %collective-permute-start.68 = (bf16[128,1536]{1,0:T(8,128)(2,1)S(1)}, bf16[128,1536]{1,0:T(8,128)(2,1)S(1)}, u32[]{:S(2)}, u32[]{:S(2)}) collective-permute-start(bf16[128,1536]{1,0:T(8,128)(2,1)S(1)} %fusion.15), channel_id=1, source_target_pairs={{0,8},{4,12},{8,0},{12,4},{16,24},{20,28},{24,16},{28,20},{1,9},{5... | collective-permute-start | bytes 1179656 | tf_op jit(solution)/shard_map/ppermute | solution.py:519
  533.5 6.3 collective-permute-done.68
  543.0 2.0 pad_maximum_fusion.11
  547.3 2.0 collective-permute-start.80
  552.6 20.8 %collective-permute-done.74 = f32[3584]{0:T(1024)S(1)} collective-permute-done((f32[3584]{0:T(1024)S(1)}, f32[3584]{0:T(1024)S(1)}, u32[]{:S(2)}, u32[]{:S(2)}) %collective-permute-start.74) | collective-permute-done | bytes 14368 | tf_op jit(solution)/shard_map/ppermute | solution.py:519
  573.7 2.5 collective-permute-start.84
  578.3 3.9 collective-permute-done.76
  582.8 6.1 collective-permute-done.84
  589.6 2.1 fusion.2
  595.6 9.0 %spread.1 = (f32[384,4096]{1,0:T(8,128)}, f32[384,4096]{1,0:T(8,128)}) custom-call(s32[8]{0:T(128)} %iota_xor_fusion.order, bf16[384,1024]{1,0:T(8,128)(2,1)} %reduce-scatter.6.cloned.1.call-done.refs_0_.refs_8_, bf16[384,1024]{1,0:T(8,128)(2,1)} %copy-done.98, bf16[384,1024]{1,0:T(8,128)(2,1)} %copy-done.91, bf16[384,1024]{1,0:T(8,128)(2,1)} %copy-done.99, ...), custom_call_target="tpu_custom_call" | custom-call | tf_op jit(solution)/shard_map/spread/pallas_call | solution.py:451
  604.6 5.5 convert_element_type.382
  610.1 15.4 %all-gather.17.cloned.1.call-done = bf16[4608,384]{1,0:T(8,128)(2,1)} async-done(((bf16[576,384]{1,0:T(8,128)(2,1)}), bf16[4608,384]{1,0:T(8,128)(2,1)}) %all-gather.17.cloned.1.call-update) | async-done | bytes 3538960 | tf_op jit(solution)/shard_map/all_gather | solution.py:769
  625.5 2.0 copy-done.47
  627.5 5.8 shard_map.236
  (593 shorter events, 192.7 us)
Async XLA Ops:
  7.2 60.9 %all-gather.13.cloned.1.call-start = ((), (), s32[]{:S(2)}) async-start(), calls=%async_computation.8 | async-start | bytes 1536000 | tf_op jit(solution)/shard_map/all_gather | solution.py:644
  10.9 120.0 %all-gather.15.cloned.1.call-start = ((), (), s32[]{:S(2)}) async-start(), calls=%async_computation.9 | async-start | bytes 2703360 | tf_op jit(solution)/shard_map/all_gather | solution.py:654
  17.2 206.6 %all-gather.9.cloned.1.call-start = ((), (), s32[]{:S(2)}) async-start(), calls=%async_computation.3 | async-start | bytes 3932160 | tf_op jit(solution)/shard_map/all_gather | solution.py:663
  17.2 34.6 %collective-permute-start.2 = (bf16[256,1536]{1,0:T(8,128)(2,1)S(1)}, bf16[256,1536]{1,0:T(8,128)(2,1)}, u32[]{:S(2)}, u32[]{:S(2)}) collective-permute-start(bf16[256,1536]{1,0:T(8,128)(2,1)S(1)} %bitcast.96), channel_id=1, source_target_pairs={{0,16},{4,20},{8,24},{12,28},{16,0},{20,4},{24,8},{28,12},{1,17},{... | collective-permute-start | bytes 2359304 | tf_op jit(solution)/shard_map/ppermute | solution.py:519
  32.1 19.8 %collective-permute-start.1 = (bf16[256,1536]{1,0:T(8,128)(2,1)S(1)}, bf16[256,1536]{1,0:T(8,128)(2,1)S(1)}, u32[]{:S(2)}, u32[]{:S(2)}) collective-permute-start(bf16[256,1536]{1,0:T(8,128)(2,1)S(1)} %bitcast.97), channel_id=1, source_target_pairs={{0,8},{4,12},{8,0},{12,4},{16,24},{20,28},{24,16},{28,20},{1,9},{5... | collective-permute-start | bytes 2359304 | tf_op jit(solution)/shard_map/ppermute | solution.py:519
  38.7 33.3 %collective-permute-start = (bf16[256,1536]{1,0:T(8,128)(2,1)S(1)}, bf16[256,1536]{1,0:T(8,128)(2,1)}, u32[]{:S(2)}, u32[]{:S(2)}) collective-permute-start(bf16[256,1536]{1,0:T(8,128)(2,1)S(1)} %bitcast.98), channel_id=1, source_target_pairs={{0,4},{4,0},{8,12},{12,8},{16,20},{20,16},{24,28},{28,24},{1,5},{5... | collective-permute-start | bytes 2359304 | tf_op jit(solution)/shard_map/ppermute | solution.py:519
  44.0 399.2 %reduce-scatter.8.cloned.1.call-start = ((), (), s32[]{:S(2)}) async-start(), calls=%async_computation.6 | async-start | bytes 1966080 | tf_op jit(solution)/shard_map/reduce_scatter | solution.py:724
  55.2 26.2 %collective-permute-start.3 = (bf16[256,1536]{1,0:T(8,128)(2,1)S(1)}, bf16[256,1536]{1,0:T(8,128)(2,1)}, u32[]{:S(2)}, u32[]{:S(2)}) collective-permute-start(bf16[256,1536]{1,0:T(8,128)(2,1)S(1)} %collective-permute-done.1.even), channel_id=1, source_target_pairs={{0,4},{4,0},{8,12},{12,8},{16,20},{20,16},{24,28},{28,24},{1,5},{5... | collective-permute-start | bytes 2359304 | tf_op jit(solution)/shard_map/ppermute | solution.py:519
  55.4 20.6 %collective-permute-start.4 = (bf16[256,1536]{1,0:T(8,128)(2,1)}, bf16[256,1536]{1,0:T(8,128)(2,1)}, u32[]{:S(2)}, u32[]{:S(2)}) collective-permute-start(bf16[256,1536]{1,0:T(8,128)(2,1)} %collective-permute-done.2.even), channel_id=1, source_target_pairs={{0,4},{4,0},{8,12},{12,8},{16,20},{20,16},{24,28},{28,24},{1,5},{5... | collective-permute-start | bytes 2359304 | tf_op jit(solution)/shard_map/ppermute | solution.py:519
  66.1 19.6 %collective-permute-start.7 = (bf16[256,1536]{1,0:T(8,128)(2,1)}, bf16[256,1536]{1,0:T(8,128)(2,1)}, u32[]{:S(2)}, u32[]{:S(2)}) collective-permute-start(bf16[256,1536]{1,0:T(8,128)(2,1)} %constant_dynamic-update-slice_fusion.even), channel_id=1, source_target_pairs={{0,4},{4,0},{8,12},{12,8},{16,20},{20,16},{24,28},{28,24},{1,5},{5... | collective-permute-start | bytes 2359304 | tf_op jit(solution)/shard_map/ppermute | solution.py:519
  66.1 100.6 %collective-permute-start.32 = (bf16[256,1536]{1,0:T(8,128)(2,1)}, bf16[256,1536]{1,0:T(8,128)(2,1)}, u32[]{:S(2)}, u32[]{:S(2)}) collective-permute-start(bf16[256,1536]{1,0:T(8,128)(2,1)} %bitcast.11.cot_even), channel_id=1, source_target_pairs={{0,16},{4,20},{8,24},{12,28},{16,0},{20,4},{24,8},{28,12},{1,17},{... | collective-permute-start | bytes 2359304 | tf_op jit(solution)/shard_map/ppermute | solution.py:519
  140.9 29.5 %collective-permute-start.9 = (bf16[256,1536]{1,0:T(8,128)(2,1)}, bf16[256,1536]{1,0:T(8,128)(2,1)}, u32[]{:S(2)}, u32[]{:S(2)}) collective-permute-start(bf16[256,1536]{1,0:T(8,128)(2,1)} %convolution_convert_fusion.5), channel_id=1, source_target_pairs={{0,4},{4,0},{8,12},{12,8},{16,20},{20,16},{24,28},{28,24},{1,5},{5... | collective-permute-start | bytes 2359304 | tf_op jit(solution)/shard_map/ppermute | solution.py:519
  141.8 12.1 %collective-permute-start.14 = (bf16[128,1536]{1,0:T(8,128)(2,1)S(1)}, bf16[128,1536]{1,0:T(8,128)(2,1)S(1)}, u32[]{:S(2)}, u32[]{:S(2)}) collective-permute-start(bf16[128,1536]{1,0:T(8,128)(2,1)S(1)} %get-tuple-element.237), channel_id=1, source_target_pairs={{0,8},{4,12},{8,0},{12,4},{16,24},{20,28},{24,16},{28,20},{1,9},{5... | collective-permute-start | bytes 1179656 | tf_op jit(solution)/shard_map/ppermute | solution.py:519
  144.2 28.9 %collective-permute-start.11 = (bf16[128,1536]{1,0:T(8,128)(2,1)}, bf16[128,1536]{1,0:T(8,128)(2,1)}, u32[]{:S(2)}, u32[]{:S(2)}) collective-permute-start(bf16[128,1536]{1,0:T(8,128)(2,1)} %slice.654), channel_id=1, source_target_pairs={{0,8},{4,12},{8,0},{12,4},{16,24},{20,28},{24,16},{28,20},{1,9},{5... | collective-permute-start | bytes 1179656 | tf_op jit(solution)/shard_map/ppermute | solution.py:519
  146.2 26.9 %collective-permute-start.18 = (bf16[128,1536]{1,0:T(8,128)(2,1)}, bf16[128,1536]{1,0:T(8,128)(2,1)}, u32[]{:S(2)}, u32[]{:S(2)}) collective-permute-start(bf16[128,1536]{1,0:T(8,128)(2,1)} %slice.653), channel_id=1, source_target_pairs={{0,16},{4,20},{8,24},{12,28},{16,0},{20,4},{24,8},{28,12},{1,17},{... | collective-permute-start | bytes 1179656 | tf_op jit(solution)/shard_map/ppermute | solution.py:519
  166.7 12.3 %collective-permute-start.17 = (bf16[128,1536]{1,0:T(8,128)(2,1)}, bf16[128,1536]{1,0:T(8,128)(2,1)}, u32[]{:S(2)}, u32[]{:S(2)}) collective-permute-start(bf16[128,1536]{1,0:T(8,128)(2,1)} %fusion.25), channel_id=1, source_target_pairs={{0,8},{4,12},{8,0},{12,4},{16,24},{20,28},{24,16},{28,20},{1,9},{5... | collective-permute-start | bytes 1179656 | tf_op jit(solution)/shard_map/ppermute | solution.py:519
  170.4 25.5 %collective-permute-start.24 = (bf16[256,1536]{1,0:T(8,128)(2,1)}, bf16[256,1536]{1,0:T(8,128)(2,1)}, u32[]{:S(2)}, u32[]{:S(2)}) collective-permute-start(bf16[256,1536]{1,0:T(8,128)(2,1)} %bitcast.11.cot_even), channel_id=1, source_target_pairs={{0,8},{4,12},{8,0},{12,4},{16,24},{20,28},{24,16},{28,20},{1,9},{5... | collective-permute-start | bytes 2359304 | tf_op jit(solution)/shard_map/ppermute | solution.py:519
  173.1 49.0 %collective-permute-start.20 = (bf16[256,1536]{1,0:T(8,128)(2,1)}, bf16[256,1536]{1,0:T(8,128)(2,1)}, u32[]{:S(2)}, u32[]{:S(2)}) collective-permute-start(bf16[256,1536]{1,0:T(8,128)(2,1)} %bitcast.11.cot_even), channel_id=1, source_target_pairs={{0,4},{4,0},{8,12},{12,8},{16,20},{20,16},{24,28},{28,24},{1,5},{5... | collective-permute-start | bytes 2359304 | tf_op jit(solution)/shard_map/ppermute | solution.py:519
  173.2 31.1 %collective-permute-start.33 = (bf16[128,1536]{1,0:T(8,128)(2,1)}, bf16[128,1536]{1,0:T(8,128)(2,1)}, u32[]{:S(2)}, u32[]{:S(2)}) collective-permute-start(bf16[128,1536]{1,0:T(8,128)(2,1)} %slice.487), channel_id=1, source_target_pairs={{0,8},{4,12},{8,0},{12,4},{16,24},{20,28},{24,16},{28,20},{1,9},{5... | collective-permute-start | bytes 1179656 | tf_op jit(solution)/shard_map/ppermute | solution.py:519
  184.0 32.8 %collective-permute-start.28 = (bf16[256,1536]{1,0:T(8,128)(2,1)}, bf16[256,1536]{1,0:T(8,128)(2,1)}, u32[]{:S(2)}, u32[]{:S(2)}) collective-permute-start(bf16[256,1536]{1,0:T(8,128)(2,1)} %multiply_convert_fusion.feed_even.refs_0_), channel_id=1, source_target_pairs={{0,16},{4,20},{8,24},{12,28},{16,0},{20,4},{24,8},{28,12},{1,17},{... | collective-permute-start | bytes 2359304 | tf_op jit(solution)/shard_map/ppermute | solution.py:519
  185.7 33.4 %collective-permute-start.22 = (bf16[256,1536]{1,0:T(8,128)(2,1)}, bf16[256,1536]{1,0:T(8,128)(2,1)}, u32[]{:S(2)}, u32[]{:S(2)}) collective-permute-start(bf16[256,1536]{1,0:T(8,128)(2,1)} %multiply_convert_fusion.feed_even.refs_0_), channel_id=1, source_target_pairs={{0,8},{4,12},{8,0},{12,4},{16,24},{20,28},{24,16},{28,20},{1,9},{5... | collective-permute-start | bytes 2359304 | tf_op jit(solution)/shard_map/ppermute | solution.py:519
  195.8 27.9 %collective-permute-start.19 = (bf16[256,1536]{1,0:T(8,128)(2,1)}, bf16[256,1536]{1,0:T(8,128)(2,1)}, u32[]{:S(2)}, u32[]{:S(2)}) collective-permute-start(bf16[256,1536]{1,0:T(8,128)(2,1)} %multiply_convert_fusion.feed_even.refs_0_), channel_id=1, source_target_pairs={{0,4},{4,0},{8,12},{12,8},{16,20},{20,16},{24,28},{28,24},{1,5},{5... | collective-permute-start | bytes 2359304 | tf_op jit(solution)/shard_map/ppermute | solution.py:519
  213.3 36.9 %collective-permute-start.39 = (bf16[256,1536]{1,0:T(8,128)(2,1)}, bf16[256,1536]{1,0:T(8,128)(2,1)}, u32[]{:S(2)}, u32[]{:S(2)}) collective-permute-start(bf16[256,1536]{1,0:T(8,128)(2,1)} %collective-permute-done.32.cot_even), channel_id=1, source_target_pairs={{0,4},{4,0},{8,12},{12,8},{16,20},{20,16},{24,28},{28,24},{1,5},{5... | collective-permute-start | bytes 2359304 | tf_op jit(solution)/shard_map/ppermute | solution.py:519
  216.9 21.3 %collective-permute-start.25 = (bf16[256,1536]{1,0:T(8,128)(2,1)}, bf16[256,1536]{1,0:T(8,128)(2,1)}, u32[]{:S(2)}, u32[]{:S(2)}) collective-permute-start(bf16[256,1536]{1,0:T(8,128)(2,1)} %collective-permute-done.24.cot_even), channel_id=1, source_target_pairs={{0,4},{4,0},{8,12},{12,8},{16,20},{20,16},{24,28},{28,24},{1,5},{5... | collective-permute-start | bytes 2359304 | tf_op jit(solution)/shard_map/ppermute | solution.py:519
  219.1 16.3 %collective-permute-start.29 = (bf16[128,1536]{1,0:T(8,128)(2,1)}, bf16[128,1536]{1,0:T(8,128)(2,1)}, u32[]{:S(2)}, u32[]{:S(2)}) collective-permute-start(bf16[128,1536]{1,0:T(8,128)(2,1)} %slice.485), channel_id=1, source_target_pairs={{0,8},{4,12},{8,0},{12,4},{16,24},{20,28},{24,16},{28,20},{1,9},{5... | collective-permute-start | bytes 1179656 | tf_op jit(solution)/shard_map/ppermute | solution.py:519
  222.0 15.0 %collective-permute-start.30 = (bf16[128,1536]{1,0:T(8,128)(2,1)}, bf16[128,1536]{1,0:T(8,128)(2,1)}, u32[]{:S(2)}, u32[]{:S(2)}) collective-permute-start(bf16[128,1536]{1,0:T(8,128)(2,1)} %slice.486), channel_id=1, source_target_pairs={{0,16},{4,20},{8,24},{12,28},{16,0},{20,4},{24,8},{28,12},{1,17},{... | collective-permute-start | bytes 1179656 | tf_op jit(solution)/shard_map/ppermute | solution.py:519
  223.8 14.9 %collective-permute-start.23 = (bf16[256,1536]{1,0:T(8,128)(2,1)}, bf16[256,1536]{1,0:T(8,128)(2,1)}, u32[]{:S(2)}, u32[]{:S(2)}) collective-permute-start(bf16[256,1536]{1,0:T(8,128)(2,1)} %collective-permute-done.22.feed_even.refs_2_), channel_id=1, source_target_pairs={{0,4},{4,0},{8,12},{12,8},{16,20},{20,16},{24,28},{28,24},{1,5},{5... | collective-permute-start | bytes 2359304 | tf_op jit(solution)/shard_map/ppermute | solution.py:519
  235.5 15.1 %collective-permute-start.38 = (bf16[256,1536]{1,0:T(8,128)(2,1)}, bf16[256,1536]{1,0:T(8,128)(2,1)S(1)}, u32[]{:S(2)}, u32[]{:S(2)}) collective-permute-start(bf16[256,1536]{1,0:T(8,128)(2,1)} %collective-permute-done.28.feed_even.refs_4_), channel_id=1, source_target_pairs={{0,4},{4,0},{8,12},{12,8},{16,20},{20,16},{24,28},{28,24},{1,5},{5... | collective-permute-start | bytes 2359304 | tf_op jit(solution)/shard_map/ppermute | solution.py:519
  237.0 24.7 %collective-permute-start.35 = (bf16[256,1536]{1,0:T(8,128)(2,1)}, bf16[256,1536]{1,0:T(8,128)(2,1)S(1)}, u32[]{:S(2)}, u32[]{:S(2)}) collective-permute-start(bf16[256,1536]{1,0:T(8,128)(2,1)} %constant_dynamic-update-slice_fusion.5.cot_even), channel_id=1, source_target_pairs={{0,4},{4,0},{8,12},{12,8},{16,20},{20,16},{24,28},{28,24},{1,5},{5... | collective-permute-start | bytes 2359304 | tf_op jit(solution)/shard_map/ppermute | solution.py:519
  238.1 93.2 %collective-permute-start.21 = (bf16[256,1536]{1,0:T(8,128)(2,1)}, bf16[256,1536]{1,0:T(8,128)(2,1)}, u32[]{:S(2)}, u32[]{:S(2)}) collective-permute-start(bf16[256,1536]{1,0:T(8,128)(2,1)} %get-tuple-element.120), channel_id=1, source_target_pairs={{0,4},{4,0},{8,12},{12,8},{16,20},{20,16},{24,28},{28,24},{1,5},{5... | collective-permute-start | bytes 2359304 | tf_op jit(solution)/shard_map/ppermute | solution.py:519
  238.7 23.0 %collective-permute-start.31 = (bf16[256,1536]{1,0:T(8,128)(2,1)S(1)}, bf16[256,1536]{1,0:T(8,128)(2,1)S(1)}, u32[]{:S(2)}, u32[]{:S(2)}) collective-permute-start(bf16[256,1536]{1,0:T(8,128)(2,1)S(1)} %constant_dynamic-update-slice_fusion.3.feed_even.refs_6_), channel_id=1, source_target_pairs={{0,4},{4,0},{8,12},{12,8},{16,20},{20,16},{24,28},{28,24},{1,5},{5... | collective-permute-start | bytes 2359304 | tf_op jit(solution)/shard_map/ppermute | solution.py:519
  250.1 56.6 %collective-permute-start.26 = (bf16[256,1536]{1,0:T(8,128)(2,1)}, bf16[256,1536]{1,0:T(8,128)(2,1)}, u32[]{:S(2)}, u32[]{:S(2)}) collective-permute-start(bf16[256,1536]{1,0:T(8,128)(2,1)} %get-tuple-element.122), channel_id=1, source_target_pairs={{0,4},{4,0},{8,12},{12,8},{16,20},{20,16},{24,28},{28,24},{1,5},{5... | collective-permute-start | bytes 2359304 | tf_op jit(solution)/shard_map/ppermute | solution.py:519
  259.6 52.6 %collective-permute-start.40 = (bf16[256,1536]{1,0:T(8,128)(2,1)}, bf16[256,1536]{1,0:T(8,128)(2,1)}, u32[]{:S(2)}, u32[]{:S(2)}) collective-permute-start(bf16[256,1536]{1,0:T(8,128)(2,1)} %get-tuple-element.126), channel_id=1, source_target_pairs={{0,4},{4,0},{8,12},{12,8},{16,20},{20,16},{24,28},{28,24},{1,5},{5... | collective-permute-start | bytes 2359304 | tf_op jit(solution)/shard_map/ppermute | solution.py:519
  274.1 36.2 %collective-permute-start.36 = (bf16[256,1536]{1,0:T(8,128)(2,1)}, bf16[256,1536]{1,0:T(8,128)(2,1)}, u32[]{:S(2)}, u32[]{:S(2)}) collective-permute-start(bf16[256,1536]{1,0:T(8,128)(2,1)} %get-tuple-element.124), channel_id=1, source_target_pairs={{0,4},{4,0},{8,12},{12,8},{16,20},{20,16},{24,28},{28,24},{1,5},{5... | collective-permute-start | bytes 2359304 | tf_op jit(solution)/shard_map/ppermute | solution.py:519
  309.5 24.4 %collective-permute-start.27 = (bf16[128,1536]{1,0:T(8,128)(2,1)}, bf16[128,1536]{1,0:T(8,128)(2,1)}, u32[]{:S(2)}, u32[]{:S(2)}) collective-permute-start(bf16[128,1536]{1,0:T(8,128)(2,1)} %slice.652), channel_id=1, source_target_pairs={{0,8},{4,12},{8,0},{12,4},{16,24},{20,28},{24,16},{28,20},{1,9},{5... | collective-permute-start | bytes 1179656 | tf_op jit(solution)/shard_map/ppermute | solution.py:519
  311.8 12.1 %collective-permute-start.37 = (bf16[128,1536]{1,0:T(8,128)(2,1)S(1)}, bf16[128,1536]{1,0:T(8,128)(2,1)S(1)}, u32[]{:S(2)}, u32[]{:S(2)}) collective-permute-start(bf16[128,1536]{1,0:T(8,128)(2,1)S(1)} %get-tuple-element.236), channel_id=1, source_target_pairs={{0,16},{4,20},{8,24},{12,28},{16,0},{20,4},{24,8},{28,12},{1,17},{... | collective-permute-start | bytes 1179656 | tf_op jit(solution)/shard_map/ppermute | solution.py:519
  315.3 18.7 %collective-permute-start.44 = (bf16[128,1536]{1,0:T(8,128)(2,1)}, bf16[128,1536]{1,0:T(8,128)(2,1)}, u32[]{:S(2)}, u32[]{:S(2)}) collective-permute-start(bf16[128,1536]{1,0:T(8,128)(2,1)} %slice.651), channel_id=1, source_target_pairs={{0,16},{4,20},{8,24},{12,28},{16,0},{20,4},{24,8},{28,12},{1,17},{... | collective-permute-start | bytes 1179656 | tf_op jit(solution)/shard_map/ppermute | solution.py:519
  316.0 13.3 %collective-permute-start.41 = (bf16[128,1536]{1,0:T(8,128)(2,1)S(1)}, bf16[128,1536]{1,0:T(8,128)(2,1)S(1)}, u32[]{:S(2)}, u32[]{:S(2)}) collective-permute-start(bf16[128,1536]{1,0:T(8,128)(2,1)S(1)} %get-tuple-element.235), channel_id=1, source_target_pairs={{0,8},{4,12},{8,0},{12,4},{16,24},{20,28},{24,16},{28,20},{1,9},{5... | collective-permute-start | bytes 1179656 | tf_op jit(solution)/shard_map/ppermute | solution.py:519
  333.9 160.0 %reduce-scatter.4.cloned.1.call-start = ((), (), s32[]{:S(2)}) async-start(), calls=%async_computation.4 | async-start | bytes 2211840 | tf_op jit(solution)/shard_map/reduce_scatter | solution.py:766
  346.0 18.2 %collective-permute-start.48 = (bf16[256,1536]{1,0:T(8,128)(2,1)S(1)}, bf16[256,1536]{1,0:T(8,128)(2,1)S(1)}, u32[]{:S(2)}, u32[]{:S(2)}) collective-permute-start(bf16[256,1536]{1,0:T(8,128)(2,1)S(1)} %subtract_add_fusion.refs_8_), channel_id=1, source_target_pairs={{0,16},{4,20},{8,24},{12,28},{16,0},{20,4},{24,8},{28,12},{1,17},{... | collective-permute-start | bytes 2359304 | tf_op jit(solution)/shard_map/ppermute | solution.py:519
  347.8 18.3 %collective-permute-start.46 = (bf16[256,1536]{1,0:T(8,128)(2,1)S(1)}, bf16[256,1536]{1,0:T(8,128)(2,1)S(1)}, u32[]{:S(2)}, u32[]{:S(2)}) collective-permute-start(bf16[256,1536]{1,0:T(8,128)(2,1)S(1)} %subtract_add_fusion.refs_8_), channel_id=1, source_target_pairs={{0,8},{4,12},{8,0},{12,4},{16,24},{20,28},{24,16},{28,20},{1,9},{5... | collective-permute-start | bytes 2359304 | tf_op jit(solution)/shard_map/ppermute | solution.py:519
  348.6 19.5 %collective-permute-start.45 = (bf16[256,1536]{1,0:T(8,128)(2,1)S(1)}, bf16[256,1536]{1,0:T(8,128)(2,1)S(1)}, u32[]{:S(2)}, u32[]{:S(2)}) collective-permute-start(bf16[256,1536]{1,0:T(8,128)(2,1)S(1)} %subtract_add_fusion.refs_8_), channel_id=1, source_target_pairs={{0,4},{4,0},{8,12},{12,8},{16,20},{20,16},{24,28},{28,24},{1,5},{5... | collective-permute-start | bytes 2359304 | tf_op jit(solution)/shard_map/ppermute | solution.py:519
  434.9 110.8 %reduce-scatter.6.cloned.1.call-start = ((), (), s32[]{:S(2)}) async-start(), calls=%async_computation.5 | async-start | bytes 3932160 | tf_op jit(solution)/shard_map/reduce_scatter | solution.py:723
  435.5 169.1 %all-gather.11.cloned.1.call-start = ((), (), s32[]{:S(2)}) async-start(), calls=%async_computation.7 | async-start | bytes 3538944 | tf_op jit(solution)/shard_map/all_gather | solution.py:731
  439.1 15.8 %collective-permute-start.63 = (bf16[256,1536]{1,0:T(8,128)(2,1)}, bf16[256,1536]{1,0:T(8,128)(2,1)}, u32[]{:S(2)}, u32[]{:S(2)}) collective-permute-start(bf16[256,1536]{1,0:T(8,128)(2,1)} %convolution_convert_fusion.6), channel_id=1, source_target_pairs={{0,4},{4,0},{8,12},{12,8},{16,20},{20,16},{24,28},{28,24},{1,5},{5... | collective-permute-start | bytes 2359304 | tf_op jit(solution)/shard_map/ppermute | solution.py:519
  441.2 17.2 %collective-permute-start.62 = (bf16[256,1536]{1,0:T(8,128)(2,1)}, bf16[256,1536]{1,0:T(8,128)(2,1)}, u32[]{:S(2)}, u32[]{:S(2)}) collective-permute-start(bf16[256,1536]{1,0:T(8,128)(2,1)} %convolution_convert_fusion.7), channel_id=1, source_target_pairs={{0,4},{4,0},{8,12},{12,8},{16,20},{20,16},{24,28},{28,24},{1,5},{5... | collective-permute-start | bytes 2359304 | tf_op jit(solution)/shard_map/ppermute | solution.py:519
  442.7 18.4 %collective-permute-start.61 = (bf16[256,1536]{1,0:T(8,128)(2,1)}, bf16[256,1536]{1,0:T(8,128)(2,1)}, u32[]{:S(2)}, u32[]{:S(2)}) collective-permute-start(bf16[256,1536]{1,0:T(8,128)(2,1)} %convolution_convert_fusion.8), channel_id=1, source_target_pairs={{0,4},{4,0},{8,12},{12,8},{16,20},{20,16},{24,28},{28,24},{1,5},{5... | collective-permute-start | bytes 2359304 | tf_op jit(solution)/shard_map/ppermute | solution.py:519
  443.2 182.3 %all-gather.17.cloned.1.call-start = ((), (), s32[]{:S(2)}) async-start(), calls=%async_computation.10 | async-start | bytes 3981312 | tf_op jit(solution)/shard_map/all_gather | solution.py:769
  467.6 37.1 %collective-permute-start.65 = (bf16[128,1536]{1,0:T(8,128)(2,1)}, bf16[128,1536]{1,0:T(8,128)(2,1)}, u32[]{:S(2)}, u32[]{:S(2)}) collective-permute-start(bf16[128,1536]{1,0:T(8,128)(2,1)} %get-tuple-element.167), channel_id=1, source_target_pairs={{0,8},{4,12},{8,0},{12,4},{16,24},{20,28},{24,16},{28,20},{1,9},{5... | collective-permute-start | bytes 1179656 | tf_op jit(solution)/shard_map/ppermute | solution.py:519
  469.8 24.0 %collective-permute-start.58 = (bf16[128,1536]{1,0:T(8,128)(2,1)S(1)}, bf16[128,1536]{1,0:T(8,128)(2,1)S(1)}, u32[]{:S(2)}, u32[]{:S(2)}) collective-permute-start(bf16[128,1536]{1,0:T(8,128)(2,1)S(1)} %slice.650), channel_id=1, source_target_pairs={{0,8},{4,12},{8,0},{12,4},{16,24},{20,28},{24,16},{28,20},{1,9},{5... | collective-permute-start | bytes 1179656 | tf_op jit(solution)/shard_map/ppermute | solution.py:519
  471.0 22.9 %collective-permute-start.59 = (bf16[128,1536]{1,0:T(8,128)(2,1)S(1)}, bf16[128,1536]{1,0:T(8,128)(2,1)}, u32[]{:S(2)}, u32[]{:S(2)}) collective-permute-start(bf16[128,1536]{1,0:T(8,128)(2,1)S(1)} %slice.649), channel_id=1, source_target_pairs={{0,16},{4,20},{8,24},{12,28},{16,0},{20,4},{24,8},{28,12},{1,17},{... | collective-permute-start | bytes 1179656 | tf_op jit(solution)/shard_map/ppermute | solution.py:519
  496.4 37.0 %collective-permute-start.64 = (bf16[128,1536]{1,0:T(8,128)(2,1)}, bf16[128,1536]{1,0:T(8,128)(2,1)}, u32[]{:S(2)}, u32[]{:S(2)}) collective-permute-start(bf16[128,1536]{1,0:T(8,128)(2,1)} %slice.648), channel_id=1, source_target_pairs={{0,8},{4,12},{8,0},{12,4},{16,24},{20,28},{24,16},{28,20},{1,9},{5... | collective-permute-start | bytes 1179656 | tf_op jit(solution)/shard_map/ppermute | solution.py:519
  498.7 22.9 %collective-permute-start.67 = (bf16[128,1536]{1,0:T(8,128)(2,1)}, bf16[128,1536]{1,0:T(8,128)(2,1)}, u32[]{:S(2)}, u32[]{:S(2)}) collective-permute-start(bf16[128,1536]{1,0:T(8,128)(2,1)} %get-tuple-element.168), channel_id=1, source_target_pairs={{0,16},{4,20},{8,24},{12,28},{16,0},{20,4},{24,8},{28,12},{1,17},{... | collective-permute-start | bytes 1179656 | tf_op jit(solution)/shard_map/ppermute | solution.py:519
  502.7 30.8 %collective-permute-start.69 = (bf16[128,1536]{1,0:T(8,128)(2,1)}, bf16[128,1536]{1,0:T(8,128)(2,1)}, u32[]{:S(2)}, u32[]{:S(2)}) collective-permute-start(bf16[128,1536]{1,0:T(8,128)(2,1)} %slice.647), channel_id=1, source_target_pairs={{0,16},{4,20},{8,24},{12,28},{16,0},{20,4},{24,8},{28,12},{1,17},{... | collective-permute-start | bytes 1179656 | tf_op jit(solution)/shard_map/ppermute | solution.py:519
  503.7 19.2 %collective-permute-start.70 = (bf16[256,1536]{1,0:T(8,128)(2,1)S(1)}, bf16[256,1536]{1,0:T(8,128)(2,1)S(1)}, u32[]{:S(2)}, u32[]{:S(2)}) collective-permute-start(bf16[256,1536]{1,0:T(8,128)(2,1)S(1)} %copy-done.51), channel_id=1, source_target_pairs={{0,4},{4,0},{8,12},{12,8},{16,20},{20,16},{24,28},{28,24},{1,5},{5... | collective-permute-start | bytes 2359304 | tf_op jit(solution)/shard_map/ppermute | solution.py:519
  506.2 27.3 %collective-permute-start.66 = (bf16[128,1536]{1,0:T(8,128)(2,1)S(1)}, bf16[128,1536]{1,0:T(8,128)(2,1)S(1)}, u32[]{:S(2)}, u32[]{:S(2)}) collective-permute-start(bf16[128,1536]{1,0:T(8,128)(2,1)S(1)} %fusion.17), channel_id=1, source_target_pairs={{0,16},{4,20},{8,24},{12,28},{16,0},{20,4},{24,8},{28,12},{1,17},{... | collective-permute-start | bytes 1179656 | tf_op jit(solution)/shard_map/ppermute | solution.py:519
  522.9 16.8 %collective-permute-start.68 = (bf16[128,1536]{1,0:T(8,128)(2,1)S(1)}, bf16[128,1536]{1,0:T(8,128)(2,1)S(1)}, u32[]{:S(2)}, u32[]{:S(2)}) collective-permute-start(bf16[128,1536]{1,0:T(8,128)(2,1)S(1)} %fusion.15), channel_id=1, source_target_pairs={{0,8},{4,12},{8,0},{12,4},{16,24},{20,28},{24,16},{28,20},{1,9},{5... | collective-permute-start | bytes 1179656 | tf_op jit(solution)/shard_map/ppermute | solution.py:519
  531.2 18.2 %collective-permute-start.71 = (bf16[128,1536]{1,0:T(8,128)(2,1)}, bf16[128,1536]{1,0:T(8,128)(2,1)}, u32[]{:S(2)}, u32[]{:S(2)}) collective-permute-start(bf16[128,1536]{1,0:T(8,128)(2,1)} %fusion.20), channel_id=1, source_target_pairs={{0,16},{4,20},{8,24},{12,28},{16,0},{20,4},{24,8},{28,12},{1,17},{... | collective-permute-start | bytes 1179656 | tf_op jit(solution)/shard_map/ppermute | solution.py:519
  533.4 16.0 %collective-permute-start.72 = (bf16[128,1536]{1,0:T(8,128)(2,1)}, bf16[128,1536]{1,0:T(8,128)(2,1)}, u32[]{:S(2)}, u32[]{:S(2)}) collective-permute-start(bf16[128,1536]{1,0:T(8,128)(2,1)} %fusion.19), channel_id=1, source_target_pairs={{0,8},{4,12},{8,0},{12,4},{16,24},{20,28},{24,16},{28,20},{1,9},{5... | collective-permute-start | bytes 1179656 | tf_op jit(solution)/shard_map/ppermute | solution.py:519
  545.8 27.8 %collective-permute-start.82 = (bf16[384,1024]{1,0:T(8,128)(2,1)}, bf16[384,1024]{1,0:T(8,128)(2,1)S(1)}, u32[]{:S(2)}, u32[]{:S(2)}) collective-permute-start(bf16[384,1024]{1,0:T(8,128)(2,1)} %reduce-scatter.6.cloned.1.call-done.refs_0_.refs_8_), channel_id=1, source_target_pairs={{0,16},{4,20},{8,24},{12,28},{16,0},{20,4},{24,8},{28,12},{1,17},{... | collective-permute-start | bytes 2359304 | tf_op jit(solution)/shard_map/ppermute | solution.py:519
  547.3 26.3 %collective-permute-start.80 = (bf16[384,1024]{1,0:T(8,128)(2,1)}, bf16[384,1024]{1,0:T(8,128)(2,1)S(1)}, u32[]{:S(2)}, u32[]{:S(2)}) collective-permute-start(bf16[384,1024]{1,0:T(8,128)(2,1)} %reduce-scatter.6.cloned.1.call-done.refs_0_.refs_8_), channel_id=1, source_target_pairs={{0,8},{4,12},{8,0},{12,4},{16,24},{20,28},{24,16},{28,20},{1,9},{5... | collective-permute-start | bytes 2359304 | tf_op jit(solution)/shard_map/ppermute | solution.py:519
  552.1 21.4 %collective-permute-start.74 = (f32[3584]{0:T(1024)S(1)}, f32[3584]{0:T(1024)S(1)}, u32[]{:S(2)}, u32[]{:S(2)}) collective-permute-start(f32[3584]{0:T(1024)S(1)} %add.340), channel_id=1, source_target_pairs={{0,8},{4,12},{8,0},{12,4},{16,24},{20,28},{24,16},{28,20},{1,9},{5... | collective-permute-start | bytes 43016 | tf_op jit(solution)/shard_map/ppermute | solution.py:519
  573.7 15.3 %collective-permute-start.84 = (bf16[192,1024]{1,0:T(8,128)(2,1)S(1)}, bf16[192,1024]{1,0:T(8,128)(2,1)S(1)}, u32[]{:S(2)}, u32[]{:S(2)}) collective-permute-start(bf16[192,1024]{1,0:T(8,128)(2,1)S(1)} %slice.459), channel_id=1, source_target_pairs={{0,8},{4,12},{8,0},{12,4},{16,24},{20,28},{24,16},{28,20},{1,9},{5... | collective-permute-start | bytes 1179656 | tf_op jit(solution)/shard_map/ppermute | solution.py:519
  576.2 13.0 %collective-permute-start.85 = (bf16[192,1024]{1,0:T(8,128)(2,1)S(1)}, bf16[192,1024]{1,0:T(8,128)(2,1)S(1)}, u32[]{:S(2)}, u32[]{:S(2)}) collective-permute-start(bf16[192,1024]{1,0:T(8,128)(2,1)S(1)} %slice.460), channel_id=1, source_target_pairs={{0,16},{4,20},{8,24},{12,28},{16,0},{20,4},{24,8},{28,12},{1,17},{... | collective-permute-start | bytes 1179656 | tf_op jit(solution)/shard_map/ppermute | solution.py:519
  (166 other events, 1298.2 us)
Sparse Core Ops, SparseCore 0:
  11.1 37.1 all-gather.12
  50.4 47.0 all-gather.14
  99.6 62.2 all-gather.8
  334.0 35.2 reduce-scatter.7
  435.0 37.5 reduce-scatter.3
  475.4 68.2 reduce-scatter.5
  545.6 41.1 all-gather.10
  588.6 36.8 all-gather.16
